TPU v7x, 512 devices: a whole 4x4x16 slice. The times are simulated.
512 devices in a mesh: leaf: 32 (over z, core), front: 16 (over x, y).
Axes of the slice: x: 4, y: 4, z: 16, core: 2. Of those that a mesh axis runs over, the one named last changes fastest.
Arguments:
- subtree_rhs: bfloat16 [524288, 256], P(('leaf', 'front')), may hold values from -6 to 6
- subtree_inverse: bfloat16 [524288, 1024], P(('leaf', 'front')), as said below
- coupling: bfloat16 [16384, 1024], P(('leaf', 'front')), may hold values from -0.1875 to 0.1875
- rhs_top: bfloat16 [4096, 256], P(('leaf', 'front')), may hold values from -6 to 6
- rhs_mid: bfloat16 [8192, 256], P(('leaf', 'front')), may hold values from -6 to 6
- rhs_low: bfloat16 [16384, 256], P(('leaf', 'front')), may hold values from -6 to 6
- inverse_top: bfloat16 [32, 16, 8, 4096], P(None, 'front', None, 'leaf'), as said below
- inverse_mid: bfloat16 [16, 16, 16, 8192], P(None, 'front', None, 'leaf'), as said below
- inverse_low: bfloat16 [8, 16, 32, 16384], P(None, 'front', None, 'leaf'), as said below
- update_mid: bfloat16 [16, 16, 16, 2, 4096], P(None, 'front', None, None, 'leaf'), may hold values from -0.0625 to 0.0625
- update_low: bfloat16 [8, 16, 32, 2, 8192], P(None, 'front', None, None, 'leaf'), may hold values from -0.0625 to 0.0625
- front_rows: int32 [7], replicated, may hold values from 1024 to 4096, as said below
Outputs:
- solution_sub: bfloat16 [524288, 256], P(('leaf', 'front'))
- solution_top: bfloat16 [4096, 256], P(('leaf', 'front'))
- solution_mid: bfloat16 [8192, 256], P(('leaf', 'front'))
- solution_low: bfloat16 [16384, 256], P(('leaf', 'front'))
Inputs may be any that keep to these rules, and one draw needn't show every extreme that they name: `front_rows`: live rows of the seven fronts in level order; each is a multiple of 128; the root has all 4096 rows, and at least one lowest front has all 4096 rows. `subtree_inverse`: each block of 1024 rows is a lower-triangular matrix with diagonal entries from 0.6 to 1.4. `inverse_top`: each front's block D is lower triangular with diagonal entries from 0.6 to 1.4. `inverse_mid`: each front's block D is lower triangular with diagonal entries from 0.6 to 1.4. `inverse_low`: each front's block D is lower triangular with diagonal entries from 0.6 to 1.4.
All inputs are finite; a program needn't handle non-finite values.
Results may differ from a plain program's by a relative error of at most 0.025.
Values may be sent and summed in bfloat16 or wider, within the bound.
No kernel may reach another device: no remote copies, remote signals or barrier semaphores. Data moves between devices by JAX's collectives and lax.ppermute only.
A program may use at most 64 MiB of HBM per device.

v0:
```python
import jax
import jax.numpy as jnp
from jax import lax
from jax.sharding import PartitionSpec as P


def partner(array, axis, distance):
    return lax.ppermute(array, axis, [(i, i ^ 1 << distance) for i in range(lax.axis_size(axis))])


def live_mask(front_rows, heap_start, groups, pieces):
    leaf_pos = lax.axis_index("leaf")
    front_pos = lax.axis_index("front")
    member = leaf_pos % groups
    node_pos = leaf_pos // groups
    lookup = jnp.arange(front_rows.shape[0], dtype=jnp.int32)
    live_rows = jnp.sum(jnp.where(lookup == heap_start + node_pos, front_rows, 0))
    front_ways = lax.axis_size("front")
    row_offset = (member * front_ways + front_pos) * pieces
    row_ids = row_offset + jnp.arange(pieces, dtype=jnp.int32)
    return (row_ids < live_rows)[:, None]


def group_gather(block, groups):
    leaf_pos = lax.axis_index("leaf")
    gathered = lax.all_gather(block, "leaf", axis=0, tiled=True)
    start_row = leaf_pos // groups * groups * block.shape[0]
    return lax.dynamic_slice_in_dim(gathered, start_row, groups * block.shape[0], 0)


def group_reduce(partial_value, groups):
    leaf_pos = lax.axis_index("leaf")
    current = partial_value.reshape(groups, -1, partial_value.shape[-1])
    for bit_pos in reversed(range(groups.bit_length() - 1)):
        half_count = current.shape[0] // 2
        lower_half = current[:half_count]
        upper_half = current[half_count:]
        upper_bit = leaf_pos // (1 << bit_pos) % 2
        kept_half = jnp.where(upper_bit == 0, lower_half, upper_half)
        sent_half = jnp.where(upper_bit == 0, upper_half, lower_half)
        current = kept_half + partner(sent_half.astype(jnp.bfloat16), "leaf", bit_pos).astype(
            sent_half.dtype
        )
    return current[0]


def forward_front(right_block, inverse, row_mask):
    groups = inverse.shape[0]
    pieces = inverse.shape[2]
    local_inverse = inverse.reshape(groups * pieces, inverse.shape[3])
    columns = group_gather(right_block, groups)
    summed = lax.psum_scatter(
        lax.dot_general(
            local_inverse, columns, (((0,), (0,)), ((), ())), preferred_element_type=jnp.float32
        ).astype(jnp.bfloat16),
        "front",
        scatter_dimension=0,
        tiled=True,
    ).astype(jnp.float32)
    return jnp.where(row_mask, summed, 0.0).astype(jnp.bfloat16)


def forward_update(child_solved, update, parent_rhs, parent_mask):
    groups = update.shape[0]
    pieces = update.shape[2]
    half_rows = update.shape[4]
    local_update = update.reshape(groups * pieces, 2 * half_rows)
    columns = group_gather(child_solved, groups)
    products = lax.dot_general(
        local_update, columns, (((0,), (0,)), ((), ())), preferred_element_type=jnp.float32
    )
    products = products.reshape(2, half_rows, columns.shape[1])
    parity = lax.axis_index("leaf") // groups % 2
    bit_pos = groups.bit_length() - 1
    kept_half = lax.dynamic_index_in_dim(products, parity, 0, keepdims=False)
    sent_half = lax.dynamic_index_in_dim(products, 1 - parity, 0, keepdims=False)
    both_sums = kept_half + partner(sent_half.astype(jnp.bfloat16), "leaf", bit_pos).astype(
        sent_half.dtype
    )
    summed = lax.psum_scatter(
        both_sums.astype(jnp.bfloat16), "front", scatter_dimension=0, tiled=True
    ).astype(jnp.float32)
    return jnp.where(parent_mask, parent_rhs.astype(jnp.float32) - summed, 0.0).astype(jnp.bfloat16)


def backward_front(solved_block, inverse, row_mask):
    groups = inverse.shape[0]
    pieces = inverse.shape[2]
    local_inverse = inverse.reshape(groups * pieces, inverse.shape[3])

    def add_rows(running, piece_rows, start_row):
        return jnp.dot(local_inverse, piece_rows, preferred_element_type=jnp.float32)

    initial = jnp.zeros((groups * pieces, solved_block.shape[1]), jnp.float32)
    partial_value = add_rows(
        initial, lax.all_gather(solved_block, "front", axis=0, tiled=True), jnp.int32(0)
    )
    summed = group_reduce(partial_value, groups)
    return jnp.where(row_mask, summed, 0.0).astype(jnp.bfloat16)


def backward_update(child_forward, update, parent_solution, row_mask):
    groups = update.shape[0]
    pieces = update.shape[2]
    half_rows = update.shape[4]
    local_update = update.reshape(groups * pieces, 2, half_rows)
    parity = lax.axis_index("leaf") // groups % 2
    bit_pos = groups.bit_length() - 1
    sibling_block = partner(parent_solution, "leaf", bit_pos)
    own_update = lax.dynamic_index_in_dim(local_update, parity, 1, keepdims=False)
    other_update = lax.dynamic_index_in_dim(local_update, 1 - parity, 1, keepdims=False)

    def add_rows(running, pieces_pair, start_row):
        own_rows, other_rows = pieces_pair
        running = jnp.dot(own_update, own_rows, preferred_element_type=jnp.float32)
        return running + jnp.dot(other_update, other_rows, preferred_element_type=jnp.float32)

    initial = jnp.zeros((groups * pieces, parent_solution.shape[1]), jnp.float32)
    partial_value = add_rows(
        initial,
        (
            lax.all_gather(parent_solution, "front", axis=0, tiled=True),
            lax.all_gather(sibling_block, "front", axis=0, tiled=True),
        ),
        jnp.int32(0),
    )
    summed = group_reduce(partial_value, groups)
    return jnp.where(row_mask, child_forward.astype(jnp.float32) - summed, 0.0).astype(jnp.bfloat16)


def shards(
    subtree_rhs,
    subtree_inverse,
    coupling,
    rhs_top,
    rhs_mid,
    rhs_low,
    inverse_top,
    inverse_mid,
    inverse_low,
    update_mid,
    update_low,
    front_rows,
):
    below_solved = jnp.dot(subtree_inverse, subtree_rhs, preferred_element_type=jnp.float32).astype(
        jnp.bfloat16
    )
    mask_top = live_mask(front_rows, 0, inverse_top.shape[0], rhs_top.shape[0])
    mask_mid = live_mask(front_rows, 1, inverse_mid.shape[0], rhs_mid.shape[0])
    mask_low = live_mask(front_rows, 3, inverse_low.shape[0], rhs_low.shape[0])
    pushed = jnp.dot(coupling, below_solved, preferred_element_type=jnp.float32)
    right_low = jnp.where(mask_low, rhs_low.astype(jnp.float32) - pushed, 0.0).astype(jnp.bfloat16)
    forward_low = forward_front(right_low, inverse_low, mask_low)
    right_mid = forward_update(forward_low, update_low, rhs_mid, mask_mid)
    forward_mid = forward_front(right_mid, inverse_mid, mask_mid)
    right_top = forward_update(forward_mid, update_mid, rhs_top, mask_top)
    forward_top = forward_front(right_top, inverse_top, mask_top)
    solution_top = backward_front(forward_top, inverse_top, mask_top)
    residual_mid = backward_update(forward_mid, update_mid, solution_top, mask_mid)
    solution_mid = backward_front(residual_mid, inverse_mid, mask_mid)
    residual_low = backward_update(forward_low, update_low, solution_mid, mask_low)
    solution_low = backward_front(residual_low, inverse_low, mask_low)
    moved = lax.dot_general(
        coupling, solution_low, (((0,), (0,)), ((), ())), preferred_element_type=jnp.float32
    )
    shifted = (below_solved.astype(jnp.float32) - moved).astype(jnp.bfloat16)
    solution_sub = lax.dot_general(
        subtree_inverse, shifted, (((0,), (0,)), ((), ())), preferred_element_type=jnp.float32
    ).astype(jnp.bfloat16)
    return (solution_sub, solution_top, solution_mid, solution_low)


def solution(mesh):
    placed = (
        P(("leaf", "front"), None),
        P(("leaf", "front"), None),
        P(("leaf", "front"), None),
        P(("leaf", "front"), None),
        P(("leaf", "front"), None),
        P(("leaf", "front"), None),
        P(None, "front", None, "leaf"),
        P(None, "front", None, "leaf"),
        P(None, "front", None, "leaf"),
        P(None, "front", None, None, "leaf"),
        P(None, "front", None, None, "leaf"),
        P(),
    )
    return jax.shard_map(
        shards,
        mesh=mesh,
        in_specs=placed,
        out_specs=(
            P(("leaf", "front"), None),
            P(("leaf", "front"), None),
            P(("leaf", "front"), None),
            P(("leaf", "front"), None),
        ),
        check_vma=False,
    )
```

profile of v0, /device:TPU:1, one launch (start us, length us, event | category | flops | bytes accessed | tf_op | source)
XLA Modules:
  0.0 1013.0 jit_solution(10693021480637807636)
XLA Ops:
  7.3 1.5 copy-done
  8.8 1.8 convolution_convert_fusion.1
  12.2 39.0 %all_gather.36 = bf16[1024,256]{1,0:T(8,128)(2,1)S(1)} all-gather(bf16[32,256]{1,0:T(8,128)(2,1)S(1)} %fusion.8), channel_id=1, replica_groups=mesh['leaf'=32,'front'=16] {'leaf'}, dimensions={0}, use_global_device_ids=true | all-gather | bytes 540672 | tf_op jit(solution)/shard_map/all_gather | solution.py:26
  52.4 81.3 %reduce-scatter.10.cloned.1.call-done = bf16[32,256]{1,0:T(8,128)(2,1)} async-done(((bf16[512,256]{1,0:T(8,128)(2,1)}), bf16[32,256]{1,0:T(8,128)(2,1)}) %reduce-scatter.10.cloned.1.call-update) | async-done | bytes 16400 | tf_op jit(solution)/shard_map/reduce_scatter | solution.py:52
  134.5 34.5 %all_gather.37 = bf16[1024,256]{1,0:T(8,128)(2,1)S(1)} all-gather(bf16[32,256]{1,0:T(8,128)(2,1)S(1)} %select_convert_fusion.15), channel_id=1, replica_groups=mesh['leaf'=32,'front'=16] {'leaf'}, dimensions={0}, use_global_device_ids=true | all-gather | bytes 540672 | tf_op jit(solution)/shard_map/all_gather | solution.py:26
  169.9 4.7 collective-permute-start
  174.9 14.5 %collective-permute-done = bf16[256,256]{0,1:T(8,128)(2,1)} collective-permute-done((bf16[256,256]{0,1:T(8,128)(2,1)S(1)}, bf16[256,256]{0,1:T(8,128)(2,1)}, u32[]{:S(2)}, u32[]{:S(2)}) %collective-permute-start) | collective-permute-done | bytes 131104 | tf_op jit(solution)/shard_map/ppermute | solution.py:8
  191.8 80.4 %reduce-scatter.12.cloned.1.call-done = bf16[16,256]{1,0:T(8,128)(2,1)} async-done(((bf16[256,256]{1,0:T(8,128)(2,1)}), bf16[16,256]{1,0:T(8,128)(2,1)}) %reduce-scatter.12.cloned.1.call-update) | async-done | bytes 8208 | tf_op jit(solution)/shard_map/reduce_scatter | solution.py:80
  273.0 34.1 %all_gather.38 = bf16[512,256]{1,0:T(8,128)(2,1)S(1)} all-gather(bf16[16,256]{1,0:T(8,128)(2,1)S(1)} %select_convert_fusion.20), channel_id=1, replica_groups=mesh['leaf'=32,'front'=16] {'leaf'}, dimensions={0}, use_global_device_ids=true | all-gather | bytes 270336 | tf_op jit(solution)/shard_map/all_gather | solution.py:26
  308.2 80.8 %reduce-scatter.14.cloned.1.call-done = bf16[16,256]{1,0:T(8,128)(2,1)} async-done(((bf16[256,256]{1,0:T(8,128)(2,1)}), bf16[16,256]{1,0:T(8,128)(2,1)}) %reduce-scatter.14.cloned.1.call-update) | async-done | bytes 8208 | tf_op jit(solution)/shard_map/reduce_scatter | solution.py:52
  389.8 34.1 %all_gather.39 = bf16[512,256]{1,0:T(8,128)(2,1)S(1)} all-gather(bf16[16,256]{1,0:T(8,128)(2,1)S(1)} %select_convert_fusion.19), channel_id=1, replica_groups=mesh['leaf'=32,'front'=16] {'leaf'}, dimensions={0}, use_global_device_ids=true | all-gather | bytes 270336 | tf_op jit(solution)/shard_map/all_gather | solution.py:26
  424.1 8.9 collective-permute-start.1
  433.1 1.3 dynamic-slice
  435.0 3.2 collective-permute-done.1
  439.6 108.8 %all-reduce.5.cloned.1.call-done = bf16[128,256]{1,0:T(8,128)(2,1)} async-done(((bf16[128,256]{1,0:T(8,128)(2,1)}), bf16[128,256]{1,0:T(8,128)(2,1)}) %all-reduce.5.cloned.1.call-update) | async-done | bytes 65552
  549.2 33.4 %all_gather.40 = bf16[256,256]{1,0:T(8,128)(2,1)S(1)} all-gather(bf16[8,256]{1,0:T(8,128)(2,1)S(1)} %select_convert_fusion.23), channel_id=1, replica_groups=mesh['leaf'=32,'front'=16] {'leaf'}, dimensions={0}, use_global_device_ids=true | all-gather | bytes 135168 | tf_op jit(solution)/shard_map/all_gather | solution.py:26
  582.6 1.1 fusion.5
  584.5 105.7 %all-reduce.7.cloned.1.call-done = bf16[128,256]{1,0:T(8,128)(2,1)} async-done(((bf16[128,256]{1,0:T(8,128)(2,1)}), bf16[128,256]{1,0:T(8,128)(2,1)}) %all-reduce.7.cloned.1.call-update) | async-done | bytes 65552
  690.9 17.5 %all_gather.41 = bf16[128,256]{1,0:T(8,128)(2,1)S(1)} all-gather(bf16[8,256]{1,0:T(8,128)(2,1)S(1)} %select_convert_fusion.22), channel_id=1, replica_groups=mesh['leaf'=32,'front'=16] {'front'}, dimensions={0}, use_global_device_ids=true | all-gather | bytes 69632 | tf_op jit(solution)/shard_map/all_gather | solution.py:96
  708.4 1.0 convolution_bitcast_fusion.4
  709.4 12.5 %collective-permute-start.2 = (bf16[16,8,256]{2,1,0:T(8,128)(2,1)S(1)}, bf16[16,8,256]{2,1,0:T(8,128)(2,1)S(1)}, u32[]{:S(2)}, u32[]{:S(2)}) collective-permute-start(bf16[16,8,256]{2,1,0:T(8,128)(2,1)S(1)} %fusion.26), channel_id=1, source_target_pairs={{0,256},{16,272},{32,288},{48,304},{64,320},{80,336},{96,352},{112... | collective-permute-start | bytes 196616 | tf_op jit(solution)/shard_map/ppermute | solution.py:8
  722.0 1.9 collective-permute-done.2
  723.9 7.9 collective-permute-start.3
  731.9 3.9 collective-permute-done.3
  735.8 2.6 collective-permute-start.4
  738.4 2.8 collective-permute-done.4
  741.2 1.9 collective-permute-start.5
  743.2 2.5 collective-permute-done.5
  745.7 12.3 %collective-permute-start.6 = (bf16[1,8,256]{2,1,0:T(8,128)(2,1)S(1)}, bf16[1,8,256]{2,1,0:T(8,128)(2,1)S(1)}, u32[]{:S(2)}, u32[]{:S(2)}) collective-permute-start(bf16[1,8,256]{2,1,0:T(8,128)(2,1)S(1)} %select_convert_fusion.21), channel_id=1, source_target_pairs={{0,16},{16,0},{32,48},{48,32},{64,80},{80,64},{96,112},{112,96},{1... | collective-permute-start | bytes 12296 | tf_op jit(solution)/shard_map/ppermute | solution.py:8
  758.8 15.9 %all_gather.42 = bf16[128,256]{1,0:T(8,128)(2,1)S(1)} all-gather(bf16[8,256]{1,0:T(8,128)(2,1)S(1)} %fusion.40), channel_id=1, replica_groups=mesh['leaf'=32,'front'=16] {'front'}, dimensions={0}, use_global_device_ids=true | all-gather | bytes 69632 | tf_op jit(solution)/shard_map/all_gather | solution.py:122
  774.7 13.4 %collective-permute-start.7 = (bf16[8,256]{1,0:T(8,128)(2,1)S(1)}, bf16[8,256]{1,0:T(8,128)(2,1)S(1)}, u32[]{:S(2)}, u32[]{:S(2)}) collective-permute-start(bf16[8,256]{1,0:T(8,128)(2,1)S(1)} %fusion.40), channel_id=1, source_target_pairs={{0,256},{16,272},{32,288},{48,304},{64,320},{80,336},{96,352},{112... | collective-permute-start | bytes 12296 | tf_op jit(solution)/shard_map/ppermute | solution.py:8
  789.1 17.8 %all_gather.43 = bf16[128,256]{1,0:T(8,128)(2,1)S(1)} all-gather(bf16[8,256]{1,0:T(8,128)(2,1)S(1)} %collective-permute-done.7), channel_id=1, replica_groups=mesh['leaf'=32,'front'=16] {'front'}, dimensions={0}, use_global_device_ids=true | all-gather | bytes 69632 | tf_op jit(solution)/shard_map/all_gather | solution.py:123
  807.1 5.3 collective-permute-start.8
  812.5 5.2 collective-permute-done.8
  817.6 1.9 collective-permute-start.9
  819.6 3.6 collective-permute-done.9
  823.2 1.9 collective-permute-start.10
  825.2 2.9 collective-permute-done.10
  828.0 16.8 %collective-permute-start.11 = (bf16[1,16,256]{2,1,0:T(8,128)(2,1)S(1)}, bf16[1,16,256]{2,1,0:T(8,128)(2,1)S(1)}, u32[]{:S(2)}, u32[]{:S(2)}) collective-permute-start(bf16[1,16,256]{2,1,0:T(8,128)(2,1)S(1)} %select_convert_fusion.17), channel_id=1, source_target_pairs={{0,16},{16,0},{32,48},{48,32},{64,80},{80,64},{96,112},{112,96},{1... | collective-permute-start | bytes 24584 | tf_op jit(solution)/shard_map/ppermute | solution.py:8
  845.7 16.0 %all_gather.44 = bf16[256,256]{1,0:T(8,128)(2,1)S(1)} all-gather(bf16[16,256]{1,0:T(8,128)(2,1)S(1)} %fusion.39), channel_id=1, replica_groups=mesh['leaf'=32,'front'=16] {'front'}, dimensions={0}, use_global_device_ids=true | all-gather | bytes 139264 | tf_op jit(solution)/shard_map/all_gather | solution.py:96
  862.0 4.4 collective-permute-start.12
  866.4 5.5 collective-permute-done.12
  872.0 1.9 collective-permute-start.13
  873.9 5.0 collective-permute-done.13
  878.9 1.9 collective-permute-start.14
  880.9 2.5 collective-permute-done.14
  883.4 10.0 collective-permute-start.15
  894.3 17.4 %all_gather.45 = bf16[256,256]{1,0:T(8,128)(2,1)S(1)} all-gather(bf16[16,256]{1,0:T(8,128)(2,1)S(1)} %fusion.37), channel_id=1, replica_groups=mesh['leaf'=32,'front'=16] {'front'}, dimensions={0}, use_global_device_ids=true | all-gather | bytes 139264 | tf_op jit(solution)/shard_map/all_gather | solution.py:122
  911.7 3.6 collective-permute-start.16
  915.5 4.5 collective-permute-done.16
  920.0 16.0 %all_gather.46 = bf16[256,256]{1,0:T(8,128)(2,1)S(1)} all-gather(bf16[16,256]{1,0:T(8,128)(2,1)S(1)} %collective-permute-done.16), channel_id=1, replica_groups=mesh['leaf'=32,'front'=16] {'front'}, dimensions={0}, use_global_device_ids=true | all-gather | bytes 139264 | tf_op jit(solution)/shard_map/all_gather | solution.py:123
  936.2 2.1 collective-permute-start.17
  938.3 4.2 collective-permute-done.17
  942.5 1.9 collective-permute-start.18
  944.5 3.0 collective-permute-done.18
  947.5 16.4 %collective-permute-start.19 = (bf16[1,32,256]{2,1,0:T(8,128)(2,1)S(1)}, bf16[1,32,256]{2,1,0:T(8,128)(2,1)S(1)}, u32[]{:S(2)}, u32[]{:S(2)}) collective-permute-start(bf16[1,32,256]{2,1,0:T(8,128)(2,1)S(1)} %select_convert_fusion.11), channel_id=1, source_target_pairs={{0,16},{16,0},{32,48},{48,32},{64,80},{80,64},{96,112},{112,96},{1... | collective-permute-start | bytes 49160 | tf_op jit(solution)/shard_map/ppermute | solution.py:8
  964.8 17.5 %all_gather.47 = bf16[512,256]{1,0:T(8,128)(2,1)S(1)} all-gather(bf16[32,256]{1,0:T(8,128)(2,1)S(1)} %fusion.36), channel_id=1, replica_groups=mesh['leaf'=32,'front'=16] {'front'}, dimensions={0}, use_global_device_ids=true | all-gather | bytes 278528 | tf_op jit(solution)/shard_map/all_gather | solution.py:96
  982.6 1.9 collective-permute-start.20
  984.5 4.1 collective-permute-done.20
  988.7 1.9 collective-permute-start.21
  990.6 2.7 collective-permute-done.21
  993.4 10.1 collective-permute-start.22
  1004.3 1.1 fusion.2
  1005.5 1.0 copy.46
  (129 shorter events, 20.3 us)
Async XLA Ops:
  7.2 1.6 copy-start
  7.2 126.5 %reduce-scatter.10.cloned.1.call-start = ((), (), s32[]{:S(2)}) async-start(), calls=%async_computation.3 | async-start | bytes 278528 | tf_op jit(solution)/shard_map/reduce_scatter | solution.py:52
  8.8 1.9 copy-start.18
  8.8 3.2 copy-start.9
  8.8 3.2 copy-start.13
  8.8 42.4 %copy-start.1 = (bf16[8,1,32,512]{3,2,1,0:T(8,128)(2,1)S(1)}, bf16[8,1,32,512]{3,2,1,0:T(8,128)(2,1)}, u32[]{:S(2)}) copy-start(bf16[8,1,32,512]{3,2,1,0:T(8,128)(2,1)} %param.20) | copy-start | bytes 786436
  10.6 1.4 copy-start.5
  10.6 41.8 %copy-start.2 = (bf16[8,1,32,2,256]{4,3,2,1,0:T(2,128)(2,1)S(1)}, bf16[8,1,32,2,256]{4,3,2,1,0:T(2,128)(2,1)}, u32[]{:S(2)}) copy-start(bf16[8,1,32,2,256]{4,3,2,1,0:T(2,128)(2,1)} %param.22) | copy-start | bytes 786436
  52.3 219.9 %reduce-scatter.12.cloned.1.call-start = ((), (), s32[]{:S(2)}) async-start(), calls=%async_computation.4 | async-start | bytes 139264 | tf_op jit(solution)/shard_map/reduce_scatter | solution.py:80
  169.0 103.2 %copy-start.16 = (bf16[16,256]{1,0:T(8,128)(2,1)S(1)}, bf16[16,256]{1,0:T(8,128)(2,1)}, u32[]{:S(2)}) copy-start(bf16[16,256]{1,0:T(8,128)(2,1)} %param.16) | copy-start | bytes 24580
  169.3 137.9 %copy-start.7 = (bf16[16,1,16,256]{3,2,1,0:T(8,128)(2,1)S(1)}, bf16[16,1,16,256]{3,2,1,0:T(8,128)(2,1)}, u32[]{:S(2)}) copy-start(bf16[16,1,16,256]{3,2,1,0:T(8,128)(2,1)} %param.19) | copy-start | bytes 393220
  169.6 254.2 %copy-start.4 = (bf16[16,1,16,2,128]{4,3,2,1,0:T(2,128)(2,1)S(1)}, bf16[16,1,16,2,128]{4,3,2,1,0:T(2,128)(2,1)}, u32[]{:S(2)}) copy-start(bf16[16,1,16,2,128]{4,3,2,1,0:T(2,128)(2,1)} %param.21) | copy-start | bytes 393220
  169.9 378.6 %copy-start.17 = (bf16[8,256]{1,0:T(8,128)(2,1)S(1)}, bf16[8,256]{1,0:T(8,128)(2,1)}, u32[]{:S(2)}) copy-start(bf16[8,256]{1,0:T(8,128)(2,1)} %param.15) | copy-start | bytes 12292
  169.9 19.4 %collective-permute-start = (bf16[256,256]{0,1:T(8,128)(2,1)S(1)}, bf16[256,256]{0,1:T(8,128)(2,1)}, u32[]{:S(2)}, u32[]{:S(2)}) collective-permute-start(bf16[256,256]{0,1:T(8,128)(2,1)S(1)} %bitcast.156), channel_id=1, source_target_pairs={{0,128},{16,144},{32,160},{48,176},{64,192},{80,208},{96,224},{112... | collective-permute-start | bytes 393224 | tf_op jit(solution)/shard_map/ppermute | solution.py:8
  191.1 197.9 %reduce-scatter.14.cloned.1.call-start = ((), (), s32[]{:S(2)}) async-start(), calls=%async_computation.5 | async-start | bytes 139264 | tf_op jit(solution)/shard_map/reduce_scatter | solution.py:52
  308.2 240.3 %all-reduce.5.cloned.1.call-start = ((), (), s32[]{:S(2)}) async-start(), calls=%async_computation.6 | async-start | bytes 131072
  424.1 14.1 %collective-permute-start.1 = (bf16[128,256]{1,0:T(8,128)(2,1)S(1)}, bf16[128,256]{1,0:T(8,128)(2,1)S(1)}, u32[]{:S(2)}, u32[]{:S(2)}) collective-permute-start(bf16[128,256]{1,0:T(8,128)(2,1)S(1)} %fusion.25), channel_id=1, source_target_pairs={{0,256},{16,272},{32,288},{48,304},{64,320},{80,336},{96,352},{112... | collective-permute-start | bytes 196616 | tf_op jit(solution)/shard_map/ppermute | solution.py:8
  438.9 251.2 %all-reduce.7.cloned.1.call-start = ((), (), s32[]{:S(2)}) async-start(), calls=%async_computation.7 | async-start | bytes 131072
  709.4 136.3 %copy-start.12 = (bf16[16,256]{1,0:T(8,128)(2,1)S(1)}, bf16[16,256]{1,0:T(8,128)(2,1)}, u32[]{:S(2)}) copy-start(bf16[16,256]{1,0:T(8,128)(2,1)} %reduce-scatter.14.cloned.1.call-done) | copy-start | bytes 24580
  709.4 14.5 %collective-permute-start.2 = (bf16[16,8,256]{2,1,0:T(8,128)(2,1)S(1)}, bf16[16,8,256]{2,1,0:T(8,128)(2,1)S(1)}, u32[]{:S(2)}, u32[]{:S(2)}) collective-permute-start(bf16[16,8,256]{2,1,0:T(8,128)(2,1)S(1)} %fusion.26), channel_id=1, source_target_pairs={{0,256},{16,272},{32,288},{48,304},{64,320},{80,336},{96,352},{112... | collective-permute-start | bytes 196616 | tf_op jit(solution)/shard_map/ppermute | solution.py:8
  723.9 11.9 %collective-permute-start.3 = (bf16[8,8,256]{2,1,0:T(8,128)(2,1)S(1)}, bf16[8,8,256]{2,1,0:T(8,128)(2,1)S(1)}, u32[]{:S(2)}, u32[]{:S(2)}) collective-permute-start(bf16[8,8,256]{2,1,0:T(8,128)(2,1)S(1)} %select_convert_fusion.9), channel_id=1, source_target_pairs={{0,128},{16,144},{32,160},{48,176},{64,192},{80,208},{96,224},{112... | collective-permute-start | bytes 98312 | tf_op jit(solution)/shard_map/ppermute | solution.py:8
  735.8 5.4 collective-permute-start.4
  741.2 4.4 collective-permute-start.5
  745.7 13.1 %collective-permute-start.6 = (bf16[1,8,256]{2,1,0:T(8,128)(2,1)S(1)}, bf16[1,8,256]{2,1,0:T(8,128)(2,1)S(1)}, u32[]{:S(2)}, u32[]{:S(2)}) collective-permute-start(bf16[1,8,256]{2,1,0:T(8,128)(2,1)S(1)} %select_convert_fusion.21), channel_id=1, source_target_pairs={{0,16},{16,0},{32,48},{48,32},{64,80},{80,64},{96,112},{112,96},{1... | collective-permute-start | bytes 12296 | tf_op jit(solution)/shard_map/ppermute | solution.py:8
  758.8 113.1 %copy-start.15 = (bf16[8,256]{1,0:T(8,128)(2,1)}, bf16[8,256]{1,0:T(8,128)(2,1)S(1)}, u32[]{:S(2)}) copy-start(bf16[8,256]{1,0:T(8,128)(2,1)S(1)} %fusion.40) | copy-start | bytes 12292
  774.7 14.4 %collective-permute-start.7 = (bf16[8,256]{1,0:T(8,128)(2,1)S(1)}, bf16[8,256]{1,0:T(8,128)(2,1)S(1)}, u32[]{:S(2)}, u32[]{:S(2)}) collective-permute-start(bf16[8,256]{1,0:T(8,128)(2,1)S(1)} %fusion.40), channel_id=1, source_target_pairs={{0,256},{16,272},{32,288},{48,304},{64,320},{80,336},{96,352},{112... | collective-permute-start | bytes 12296 | tf_op jit(solution)/shard_map/ppermute | solution.py:8
  806.9 86.5 %copy-start.3 = (bf16[8,1,32,2,256]{4,3,2,1,0:T(2,128)(2,1)S(1)}, bf16[8,1,32,2,256]{4,3,2,1,0:T(2,128)(2,1)}, u32[]{:S(2)}) copy-start(bf16[8,1,32,2,256]{4,3,2,1,0:T(2,128)(2,1)} %param.22) | copy-start | bytes 786436
  807.1 10.5 %collective-permute-start.8 = (bf16[8,16,256]{2,1,0:T(8,128)(2,1)S(1)}, bf16[8,16,256]{2,1,0:T(8,128)(2,1)S(1)}, u32[]{:S(2)}, u32[]{:S(2)}) collective-permute-start(bf16[8,16,256]{2,1,0:T(8,128)(2,1)S(1)} %bitcast.159), channel_id=1, source_target_pairs={{0,128},{16,144},{32,160},{48,176},{64,192},{80,208},{96,224},{112... | collective-permute-start | bytes 196616 | tf_op jit(solution)/shard_map/ppermute | solution.py:8
  817.6 5.6 collective-permute-start.9
  823.2 4.8 collective-permute-start.10
  828.0 17.6 %collective-permute-start.11 = (bf16[1,16,256]{2,1,0:T(8,128)(2,1)S(1)}, bf16[1,16,256]{2,1,0:T(8,128)(2,1)S(1)}, u32[]{:S(2)}, u32[]{:S(2)}) collective-permute-start(bf16[1,16,256]{2,1,0:T(8,128)(2,1)S(1)} %select_convert_fusion.17), channel_id=1, source_target_pairs={{0,16},{16,0},{32,48},{48,32},{64,80},{80,64},{96,112},{112,96},{1... | collective-permute-start | bytes 24584 | tf_op jit(solution)/shard_map/ppermute | solution.py:8
  862.0 10.0 collective-permute-start.12
  871.9 92.8 %copy-start.8 = (bf16[32,256]{1,0:T(8,128)(2,1)S(1)}, bf16[32,256]{1,0:T(8,128)(2,1)}, u32[]{:S(2)}) copy-start(bf16[32,256]{1,0:T(8,128)(2,1)} %reduce-scatter.10.cloned.1.call-done) | copy-start | bytes 49156
  872.0 6.9 collective-permute-start.13
  878.9 4.5 collective-permute-start.14
  883.4 10.8 %collective-permute-start.15 = (bf16[1,16,256]{2,1,0:T(8,128)(2,1)S(1)}, bf16[1,16,256]{2,1,0:T(8,128)(2,1)S(1)}, u32[]{:S(2)}, u32[]{:S(2)}) collective-permute-start(bf16[1,16,256]{2,1,0:T(8,128)(2,1)S(1)} %select_convert_fusion.16), channel_id=1, source_target_pairs={{0,16},{16,0},{32,48},{48,32},{64,80},{80,64},{96,112},{112,96},{1... | collective-permute-start | bytes 24584 | tf_op jit(solution)/shard_map/ppermute | solution.py:8
  894.3 88.3 %copy-start.11 = (bf16[16,256]{1,0:T(8,128)(2,1)}, bf16[16,256]{1,0:T(8,128)(2,1)S(1)}, u32[]{:S(2)}) copy-start(bf16[16,256]{1,0:T(8,128)(2,1)S(1)} %fusion.37) | copy-start | bytes 24580
  911.7 8.3 collective-permute-start.16
  936.2 68.1 %copy-start.6 = (bf16[1024,256]{1,0:T(8,128)(2,1)S(1)}, bf16[1024,256]{1,0:T(8,128)(2,1)}, u32[]{:S(2)}) copy-start(bf16[1024,256]{1,0:T(8,128)(2,1)} %copy-done.5) | copy-start | bytes 1572868
  936.2 68.1 %copy-start.10 = (bf16[32,1024]{1,0:T(8,128)(2,1)S(1)}, bf16[32,1024]{1,0:T(8,128)(2,1)}, u32[]{:S(2)}) copy-start(bf16[32,1024]{1,0:T(8,128)(2,1)} %param.14) | copy-start | bytes 196612
  936.2 6.3 collective-permute-start.17
  942.5 5.0 collective-permute-start.18
  947.5 17.2 %collective-permute-start.19 = (bf16[1,32,256]{2,1,0:T(8,128)(2,1)S(1)}, bf16[1,32,256]{2,1,0:T(8,128)(2,1)S(1)}, u32[]{:S(2)}, u32[]{:S(2)}) collective-permute-start(bf16[1,32,256]{2,1,0:T(8,128)(2,1)S(1)} %select_convert_fusion.11), channel_id=1, source_target_pairs={{0,16},{16,0},{32,48},{48,32},{64,80},{80,64},{96,112},{112,96},{1... | collective-permute-start | bytes 49160 | tf_op jit(solution)/shard_map/ppermute | solution.py:8
  982.6 6.1 collective-permute-start.20
  988.7 4.7 collective-permute-start.21
  993.4 10.9 %collective-permute-start.22 = (bf16[1,32,256]{2,1,0:T(8,128)(2,1)S(1)}, bf16[1,32,256]{2,1,0:T(8,128)(2,1)S(1)}, u32[]{:S(2)}, u32[]{:S(2)}) collective-permute-start(bf16[1,32,256]{2,1,0:T(8,128)(2,1)S(1)} %select_convert_fusion.10), channel_id=1, source_target_pairs={{0,16},{16,0},{32,48},{48,32},{64,80},{80,64},{96,112},{112,96},{1... | collective-permute-start | bytes 49160 | tf_op jit(solution)/shard_map/ppermute | solution.py:8
  1004.3 2.2 copy-start.14
Sparse Core Ops, SparseCore 0:
  52.4 81.2 reduce-scatter.9
  191.2 81.0 reduce-scatter.11
  308.3 80.6 reduce-scatter.13
  439.0 109.3 all-reduce.4
  584.6 105.5 all-reduce.6
where the time goes:
time: 1010 us
  waiting for transfers between devices  534 us (53%)
  blocking collectives  293 us (29%)
  starting transfers between devices  147 us (15%)
  between operations  15.4 us (2%)
    unnamed x7, waiting for transfers between devices  215 us
    all_gather x5, blocking collectives, group_gather(): gathered = lax.all_gather(block, 'leaf', axis=0, tiled=True)  175 us
    reduce_scatter x2, waiting for transfers between devices, forward_front(): lax.psum_scatter(lax.dot_general(local_inverse, columns, (((0,), (0,)), (...  162 us
    ppermute x23, starting transfers between devices, partner(): lax.ppermute(array, axis, [(i, i ^ 1 << distance) for i in range(lax.axis...  146 us
    reduce_scatter x1, waiting for transfers between devices, forward_update(): lax.psum_scatter(both_sums.astype(jnp.bfloat16), 'front', scatter_dimensi...  80.4 us
    ppermute x23, waiting for transfers between devices, partner(): lax.ppermute(array, axis, [(i, i ^ 1 << distance) for i in range(lax.axis...  76.8 us
    all_gather x3, blocking collectives, backward_front(): lax.all_gather(solved_block, 'front', axis=0, tiled=True)  51 us
    all_gather x2, blocking collectives, backward_update(): lax.all_gather(sibling_block, 'front', axis=0, tiled=True)  33.8 us
  transfers between devices with their start and end apart: 28, of which 28 were waited for; matrix products, arithmetic and copies ran while one was open for 0% of the time, Pallas kernels for 0%

commit v1 on v0

v1 whole, which is shorter than its diff:
```python
import jax
import jax.numpy as jnp
from jax import lax
from jax.sharding import Mesh, PartitionSpec as P

FRONT = ("x", "y")
LEAF = ("mid", "low", "z", "core")
GROUP_AXES = {8: ("z", "core"), 16: ("low", "z", "core"), 32: ("mid", "low", "z", "core")}
SIBLING_AXIS = {8: "low", 16: "mid"}


def swap(array, axis):
    return lax.ppermute(array, axis, [(0, 1), (1, 0)])


def gather(block, axes):
    ways = lax.axis_size(axes)
    sent = jnp.broadcast_to(block[None], (ways,) + block.shape)
    got = lax.all_to_all(sent, axes, 0, 0, tiled=True)
    return got.reshape(ways * block.shape[0], block.shape[1])


def reduce_rows(partial_value, axes):
    ways = lax.axis_size(axes)
    sent = partial_value.astype(jnp.bfloat16).reshape(ways, -1, partial_value.shape[-1])
    got = lax.all_to_all(sent, axes, 0, 0, tiled=True)
    return jnp.sum(got.astype(jnp.float32), axis=0)


def live_mask(front_rows, heap_start, groups, pieces):
    leaf_pos = lax.axis_index(LEAF)
    front_pos = lax.axis_index(FRONT)
    member = leaf_pos % groups
    node_pos = leaf_pos // groups
    lookup = jnp.arange(front_rows.shape[0], dtype=jnp.int32)
    live_rows = jnp.sum(jnp.where(lookup == heap_start + node_pos, front_rows, 0))
    row_offset = (member * lax.axis_size(FRONT) + front_pos) * pieces
    row_ids = row_offset + jnp.arange(pieces, dtype=jnp.int32)
    return (row_ids < live_rows)[:, None]


def forward_front(right_block, inverse, row_mask):
    groups, _, pieces, rows = inverse.shape
    local_inverse = inverse.reshape(groups * pieces, rows)
    columns = gather(right_block, GROUP_AXES[groups])
    summed = reduce_rows(
        lax.dot_general(
            local_inverse, columns, (((0,), (0,)), ((), ())), preferred_element_type=jnp.float32
        ),
        FRONT,
    )
    return jnp.where(row_mask, summed, 0.0).astype(jnp.bfloat16)


def forward_update(child_solved, update, parent_rhs, parent_mask):
    groups, _, pieces, _, half_rows = update.shape
    local_update = update.reshape(groups * pieces, 2 * half_rows)
    columns = gather(child_solved, GROUP_AXES[groups])
    products = lax.dot_general(
        local_update, columns, (((0,), (0,)), ((), ())), preferred_element_type=jnp.float32
    ).reshape(2, lax.axis_size(FRONT), -1, columns.shape[1])
    sent = products.astype(jnp.bfloat16).transpose(1, 0, 2, 3)
    got = lax.all_to_all(sent, FRONT, 0, 0, tiled=True)
    sums = jnp.sum(got.astype(jnp.float32), axis=0)
    axis = SIBLING_AXIS[groups]
    parity = lax.axis_index(axis)
    kept = jnp.where(parity == 0, sums[0], sums[1])
    other = jnp.where(parity == 0, sums[1], sums[0])
    total = kept + swap(other.astype(jnp.bfloat16), axis).astype(jnp.float32)
    return jnp.where(parent_mask, parent_rhs.astype(jnp.float32) - total, 0.0).astype(jnp.bfloat16)


def backward_front(solved_block, inverse, row_mask):
    groups, _, pieces, rows = inverse.shape
    local_inverse = inverse.reshape(groups * pieces, rows)
    partial_value = jnp.dot(
        local_inverse, gather(solved_block, FRONT), preferred_element_type=jnp.float32
    )
    summed = reduce_rows(partial_value, GROUP_AXES[groups])
    return jnp.where(row_mask, summed, 0.0).astype(jnp.bfloat16)


def backward_update(child_forward, update, parent_solution, row_mask):
    groups, _, pieces, _, half_rows = update.shape
    local_update = update.reshape(groups * pieces, 2 * half_rows)
    axis = SIBLING_AXIS[groups]
    parity = lax.axis_index(axis)
    sibling = swap(parent_solution, axis)
    pair = jnp.stack(
        [
            jnp.where(parity == 0, parent_solution, sibling),
            jnp.where(parity == 0, sibling, parent_solution),
        ]
    )
    ways = lax.axis_size(FRONT)
    sent = jnp.broadcast_to(pair[None], (ways,) + pair.shape)
    got = lax.all_to_all(sent, FRONT, 0, 0, tiled=True)
    rows = got.transpose(1, 0, 2, 3).reshape(2 * half_rows, -1)
    partial_value = jnp.dot(local_update, rows, preferred_element_type=jnp.float32)
    summed = reduce_rows(partial_value, GROUP_AXES[groups])
    return jnp.where(row_mask, child_forward.astype(jnp.float32) - summed, 0.0).astype(jnp.bfloat16)


def shards(
    subtree_rhs,
    subtree_inverse,
    coupling,
    rhs_top,
    rhs_mid,
    rhs_low,
    inverse_top,
    inverse_mid,
    inverse_low,
    update_mid,
    update_low,
    front_rows,
):
    below_solved = jnp.dot(subtree_inverse, subtree_rhs, preferred_element_type=jnp.float32).astype(
        jnp.bfloat16
    )
    mask_top = live_mask(front_rows, 0, inverse_top.shape[0], rhs_top.shape[0])
    mask_mid = live_mask(front_rows, 1, inverse_mid.shape[0], rhs_mid.shape[0])
    mask_low = live_mask(front_rows, 3, inverse_low.shape[0], rhs_low.shape[0])
    pushed = jnp.dot(coupling, below_solved, preferred_element_type=jnp.float32)
    right_low = jnp.where(mask_low, rhs_low.astype(jnp.float32) - pushed, 0.0).astype(jnp.bfloat16)
    forward_low = forward_front(right_low, inverse_low, mask_low)
    right_mid = forward_update(forward_low, update_low, rhs_mid, mask_mid)
    forward_mid = forward_front(right_mid, inverse_mid, mask_mid)
    right_top = forward_update(forward_mid, update_mid, rhs_top, mask_top)
    forward_top = forward_front(right_top, inverse_top, mask_top)
    solution_top = backward_front(forward_top, inverse_top, mask_top)
    residual_mid = backward_update(forward_mid, update_mid, solution_top, mask_mid)
    solution_mid = backward_front(residual_mid, inverse_mid, mask_mid)
    residual_low = backward_update(forward_low, update_low, solution_mid, mask_low)
    solution_low = backward_front(residual_low, inverse_low, mask_low)
    moved = lax.dot_general(
        coupling, solution_low, (((0,), (0,)), ((), ())), preferred_element_type=jnp.float32
    )
    shifted = (below_solved.astype(jnp.float32) - moved).astype(jnp.bfloat16)
    solution_sub = lax.dot_general(
        subtree_inverse, shifted, (((0,), (0,)), ((), ())), preferred_element_type=jnp.float32
    ).astype(jnp.bfloat16)
    return (solution_sub, solution_top, solution_mid, solution_low)


def solution(mesh):
    fine = Mesh(mesh.devices.reshape(2, 2, 4, 2, 4, 4), LEAF + FRONT)
    rows = P(LEAF + FRONT, None)
    placed = (
        rows,
        rows,
        rows,
        rows,
        rows,
        rows,
        P(None, FRONT, None, LEAF),
        P(None, FRONT, None, LEAF),
        P(None, FRONT, None, LEAF),
        P(None, FRONT, None, None, LEAF),
        P(None, FRONT, None, None, LEAF),
        P(),
    )
    return jax.shard_map(
        shards, mesh=fine, in_specs=placed, out_specs=(rows, rows, rows, rows), check_vma=False
    )
```

time: 1010 us -> 337 us (0.33)
  waiting for transfers between devices: 534 us -> 40.5 us
  starting transfers between devices: 147 us -> 35.1 us
  blocking collectives: 293 us -> 245 us
  between operations: 15.4 us -> 1.11 us
    all_gather x12 -> x0, blocking collectives: 293 us -> none  [the longest x5 175 us: group_gather(): gathered = lax.all_gather(block, 'leaf', axis=0, tiled=True)]
    all_to_all x0 -> x17, blocking collectives: none -> 245 us  [the longest x7 113 us: gather(): got = lax.all_to_all(sent, axes, 0, 0, tiled=True)]
    reduce_scatter x3 -> x0, waiting for transfers between devices: 242 us -> none  [the longest x2 162 us: forward_front(): lax.psum_scatter(lax.dot_general(local_inverse, columns, (((0,), (0,)), (...]
    unnamed x7 -> x0, waiting for transfers between devices: 215 us -> none
    ppermute x23 -> x4, starting transfers between devices: 146 us -> 22.3 us  [swap(): return lax.ppermute(array, axis, [(0, 1), (1, 0)])]
    ppermute x23 -> x4, waiting for transfers between devices: 76.8 us -> 20.7 us  [swap(): return lax.ppermute(array, axis, [(0, 1), (1, 0)])]
    all_to_all x0 -> x3, waiting for transfers between devices: none -> 19.8 us  [the longest x2 14 us: forward_update(): got = lax.all_to_all(sent, FRONT, 0, 0, tiled=True)]
    all_to_all x0 -> x3, starting transfers between devices: none -> 12.7 us  [the longest x2 7.17 us: forward_update(): got = lax.all_to_all(sent, FRONT, 0, 0, tiled=True)]
  transfers between devices with their start and end apart: 28 -> 7, of which waited for: 28 -> 7; matrix products, arithmetic and copies ran while one was open for 0% -> 0% of each run, Pallas kernels for 0% -> 0%
where the time goes in v1:
time: 337 us; the launch traced here: 335 us
  blocking collectives  245 us (73%)
  waiting for transfers between devices  40.5 us (12%)
  starting transfers between devices  35.1 us (10%)
  matrix products  5.28 us (2%)
  other arithmetic  4.63 us (1%)
  local copies, waits for them, and re-layouts  3.56 us (1%)
    all_to_all x7, blocking collectives, gather(): got = lax.all_to_all(sent, axes, 0, 0, tiled=True)  113 us
    all_to_all x8, blocking collectives, reduce_rows(): got = lax.all_to_all(sent, axes, 0, 0, tiled=True)  113 us
    ppermute x4, starting transfers between devices, swap(): return lax.ppermute(array, axis, [(0, 1), (1, 0)])  22.3 us
    ppermute x4, waiting for transfers between devices, swap(): return lax.ppermute(array, axis, [(0, 1), (1, 0)])  20.7 us
    all_to_all x2, blocking collectives, backward_update(): got = lax.all_to_all(sent, FRONT, 0, 0, tiled=True)  20.2 us
    all_to_all x2, waiting for transfers between devices, forward_update(): got = lax.all_to_all(sent, FRONT, 0, 0, tiled=True)  14 us
    all_to_all x2, starting transfers between devices, forward_update(): got = lax.all_to_all(sent, FRONT, 0, 0, tiled=True)  7.17 us
  transfers between devices with their start and end apart: 7, of which 7 were waited for; matrix products, arithmetic and copies ran while one was open for 0% of the time, Pallas kernels for 0%

profile of v1, /device:TPU:1, one launch (start us, length us, event | category | flops | bytes accessed | tf_op | source)
XLA Modules:
  0.0 335.5 jit_solution(17585707708611853214)
XLA Ops:
  0.7 1.5 fusion.29
  2.2 0.7 add_compare_fusion.2
  2.9 1.8 convolution_convert_fusion.1
  4.7 0.2 fusion.9
  4.9 15.2 %all_to_all.100 = bf16[8,32,256]{2,1,0:T(8,128)(2,1)S(1)} all-to-all(bf16[8,32,256]{2,1,0:T(8,128)(2,1)S(1)} %broadcast_in_dim.140), channel_id=1, replica_groups=mesh['mid'=2,'low'=2,'z'=4,'core'=2,'x'=4,'y'=4] {'z','core'}, dimensions={0} | all-to-all | bytes 262144 | tf_op jit(solution)/shard_map/all_to_all | solution.py:19
  20.2 0.2 fusion.3
  20.4 0.1 copy.20
  20.6 12.0 %all_to_all.101 = bf16[16,32,256]{2,1,0:T(8,128)(2,1)S(1)} all-to-all(bf16[16,32,256]{2,1,0:T(8,128)(2,1)S(1)} %bitcast.144), channel_id=1, replica_groups=mesh['mid'=2,'low'=2,'z'=4,'core'=2,'x'=4,'y'=4] {'x','y'}, dimensions={0} | all-to-all | bytes 524288 | tf_op jit(solution)/shard_map/all_to_all | solution.py:26
  32.6 0.1 select_convert_fusion.2
  32.6 0.7 broadcast_in_dim.142
  33.3 5.6 %all-to-all-start.2 = ((bf16[8,32,256]{2,1,0:T(8,128)(2,1)}), bf16[8,32,256]{2,1,0:T(8,128)(2,1)S(1)}, u32[]{:S(2)}, u32[]{:S(2)}) async-start(bf16[8,32,256]{2,1,0:T(8,128)(2,1)} %broadcast_in_dim.142), calls=%async_computation.2 | async-start | bytes 262144 | tf_op jit(solution)/shard_map/all_to_all | solution.py:19
  38.9 5.8 %all-to-all-done.2 = bf16[8,32,256]{2,1,0:T(8,128)(2,1)S(1)} async-done(((bf16[8,32,256]{2,1,0:T(8,128)(2,1)}), bf16[8,32,256]{2,1,0:T(8,128)(2,1)S(1)}, u32[]{:S(2)}, u32[]{:S(2)}) %all-to-all-start.2) | async-done | bytes 131104 | tf_op jit(solution)/shard_map/all_to_all | solution.py:19
  44.7 0.2 fusion.4
  45.0 0.1 copy.21
  45.1 0.7 copy.22
  45.8 3.7 %all-to-all-start.3 = ((bf16[16,2,16,256]{3,2,1,0:T(8,128)(2,1)}), bf16[16,2,16,256]{3,2,1,0:T(8,128)(2,1)S(1)}, u32[]{:S(2)}, u32[]{:S(2)}) async-start(bf16[16,2,16,256]{3,2,1,0:T(8,128)(2,1)} %copy.22), calls=%async_computation.3 | async-start | bytes 524288 | tf_op jit(solution)/shard_map/all_to_all | solution.py:63
  49.5 7.3 %all-to-all-done.3 = bf16[16,2,16,256]{3,2,1,0:T(8,128)(2,1)S(1)} async-done(((bf16[16,2,16,256]{3,2,1,0:T(8,128)(2,1)}), bf16[16,2,16,256]{3,2,1,0:T(8,128)(2,1)S(1)}, u32[]{:S(2)}, u32[]{:S(2)}) %all-to-all-start.3) | async-done | bytes 262176 | tf_op jit(solution)/shard_map/all_to_all | solution.py:63
  56.9 8.8 %collective-permute-start = (bf16[16,256]{1,0:T(8,128)(2,1)S(1)}, bf16[16,256]{1,0:T(8,128)(2,1)S(1)}, u32[]{:S(2)}, u32[]{:S(2)}) collective-permute-start(bf16[16,256]{1,0:T(8,128)(2,1)S(1)} %fusion.22), channel_id=1, source_target_pairs={{0,128},{128,0},{1,129},{129,1},{2,130},{130,2},{3,131},{131,3},{4... | collective-permute-start | bytes 24584 | tf_op jit(solution)/shard_map/ppermute | solution.py:13
  65.7 0.7 add_compare_fusion.1
  66.4 0.4 collective-permute-done
  66.7 0.1 fusion.21
  66.8 23.0 %all_to_all.102 = bf16[16,16,256]{2,1,0:T(8,128)(2,1)S(1)} all-to-all(bf16[16,16,256]{2,1,0:T(8,128)(2,1)S(1)} %broadcast_in_dim.144), channel_id=1, replica_groups=mesh['mid'=2,'low'=2,'z'=4,'core'=2,'x'=4,'y'=4] {'low','z','core'}, dimensions={0} | all-to-all | bytes 262144 | tf_op jit(solution)/shard_map/all_to_all | solution.py:19
  89.8 0.2 convolution_convert_fusion.10
  90.0 9.8 %all_to_all.103 = bf16[16,16,256]{2,1,0:T(8,128)(2,1)S(1)} all-to-all(bf16[16,16,256]{2,1,0:T(8,128)(2,1)S(1)} %bitcast.155), channel_id=1, replica_groups=mesh['mid'=2,'low'=2,'z'=4,'core'=2,'x'=4,'y'=4] {'x','y'}, dimensions={0} | all-to-all | bytes 262144 | tf_op jit(solution)/shard_map/all_to_all | solution.py:26
  99.9 0.1 select_convert_fusion.5
  100.0 18.2 %all_to_all.104 = bf16[16,16,256]{2,1,0:T(8,128)(2,1)S(1)} all-to-all(bf16[16,16,256]{2,1,0:T(8,128)(2,1)S(1)} %broadcast_in_dim.146), channel_id=1, replica_groups=mesh['mid'=2,'low'=2,'z'=4,'core'=2,'x'=4,'y'=4] {'low','z','core'}, dimensions={0} | all-to-all | bytes 262144 | tf_op jit(solution)/shard_map/all_to_all | solution.py:19
  118.2 0.2 convolution_convert_fusion.9
  118.4 0.6 copy.40
  119.1 3.5 %all-to-all-start.7 = ((bf16[16,2,8,256]{3,2,1,0:T(8,128)(2,1)}), bf16[16,2,8,256]{3,2,1,0:T(8,128)(2,1)S(1)}, u32[]{:S(2)}, u32[]{:S(2)}) async-start(bf16[16,2,8,256]{3,2,1,0:T(8,128)(2,1)} %bitcast.138), calls=%async_computation.7 | async-start | bytes 262144 | tf_op jit(solution)/shard_map/all_to_all | solution.py:63
  122.6 6.7 %all-to-all-done.7 = bf16[16,2,8,256]{3,2,1,0:T(8,128)(2,1)S(1)} async-done(((bf16[16,2,8,256]{3,2,1,0:T(8,128)(2,1)}), bf16[16,2,8,256]{3,2,1,0:T(8,128)(2,1)S(1)}, u32[]{:S(2)}, u32[]{:S(2)}) %all-to-all-start.7) | async-done | bytes 131104 | tf_op jit(solution)/shard_map/all_to_all | solution.py:63
  129.3 7.9 %collective-permute-start.1 = (bf16[8,256]{1,0:T(8,128)(2,1)S(1)}, bf16[8,256]{1,0:T(8,128)(2,1)S(1)}, u32[]{:S(2)}, u32[]{:S(2)}) collective-permute-start(bf16[8,256]{1,0:T(8,128)(2,1)S(1)} %fusion.26), channel_id=1, source_target_pairs={{0,256},{256,0},{1,257},{257,1},{2,258},{258,2},{3,259},{259,3},{4... | collective-permute-start | bytes 12296 | tf_op jit(solution)/shard_map/ppermute | solution.py:13
  137.3 0.7 add_compare_fusion
  137.9 4.5 %collective-permute-done.1 = bf16[8,256]{1,0:T(8,128)(2,1)S(1)} collective-permute-done((bf16[8,256]{1,0:T(8,128)(2,1)S(1)}, bf16[8,256]{1,0:T(8,128)(2,1)S(1)}, u32[]{:S(2)}, u32[]{:S(2)}) %collective-permute-start.1) | collective-permute-done | bytes 4128 | tf_op jit(solution)/shard_map/ppermute | solution.py:13
  142.5 26.0 %all_to_all.105 = bf16[32,8,256]{2,1,0:T(8,128)(2,1)S(1)} all-to-all(bf16[32,8,256]{2,1,0:T(8,128)(2,1)S(1)} %broadcast_in_dim.148), channel_id=1, replica_groups=mesh['mid'=2,'low'=2,'z'=4,'core'=2,'x'=4,'y'=4] {'mid','low','z','core'}, dimensions={0} | all-to-all | bytes 262144 | tf_op jit(solution)/shard_map/all_to_all | solution.py:19
  168.5 0.2 fusion.6
  168.7 9.6 %all_to_all.106 = bf16[16,8,256]{2,1,0:T(8,128)(2,1)S(1)} all-to-all(bf16[16,8,256]{2,1,0:T(8,128)(2,1)S(1)} %fusion.6), channel_id=1, replica_groups=mesh['mid'=2,'low'=2,'z'=4,'core'=2,'x'=4,'y'=4] {'x','y'}, dimensions={0} | all-to-all | bytes 131072 | tf_op jit(solution)/shard_map/all_to_all | solution.py:26
  178.4 0.1 select_convert_fusion.8
  178.5 9.7 %all_to_all.107 = bf16[16,8,256]{2,1,0:T(8,128)(2,1)S(1)} all-to-all(bf16[16,8,256]{2,1,0:T(8,128)(2,1)S(1)} %broadcast_in_dim.149), channel_id=1, replica_groups=mesh['mid'=2,'low'=2,'z'=4,'core'=2,'x'=4,'y'=4] {'x','y'}, dimensions={0} | all-to-all | bytes 131072 | tf_op jit(solution)/shard_map/all_to_all | solution.py:19
  188.2 0.2 fusion.5
  188.4 23.0 %all_to_all.108 = bf16[32,8,256]{2,1,0:T(8,128)(2,1)S(1)} all-to-all(bf16[32,8,256]{2,1,0:T(8,128)(2,1)S(1)} %fusion.5), channel_id=1, replica_groups=mesh['mid'=2,'low'=2,'z'=4,'core'=2,'x'=4,'y'=4] {'mid','low','z','core'}, dimensions={0} | all-to-all | bytes 262144 | tf_op jit(solution)/shard_map/all_to_all | solution.py:26
  211.4 0.1 select_convert_fusion.7
  211.5 2.8 collective-permute-start.2
  214.3 10.2 %collective-permute-done.2 = bf16[8,256]{1,0:T(8,128)(2,1)S(1)} collective-permute-done((bf16[8,256]{1,0:T(8,128)(2,1)S(1)}, bf16[8,256]{1,0:T(8,128)(2,1)S(1)}, u32[]{:S(2)}, u32[]{:S(2)}) %collective-permute-start.2) | collective-permute-done | bytes 4128 | tf_op jit(solution)/shard_map/ppermute | solution.py:13
  224.6 9.6 %all_to_all.109 = bf16[16,2,8,256]{3,2,1,0:T(8,128)(2,1)S(1)} all-to-all(bf16[16,2,8,256]{3,2,1,0:T(8,128)(2,1)S(1)} %broadcast_in_dim.150), channel_id=1, replica_groups=mesh['mid'=2,'low'=2,'z'=4,'core'=2,'x'=4,'y'=4] {'x','y'}, dimensions={0} | all-to-all | bytes 262144 | tf_op jit(solution)/shard_map/all_to_all | solution.py:97
  234.3 0.2 convolution_convert_fusion.7
  234.5 18.4 %all_to_all.110 = bf16[16,16,256]{2,1,0:T(8,128)(2,1)S(1)} all-to-all(bf16[16,16,256]{2,1,0:T(8,128)(2,1)S(1)} %bitcast.159), channel_id=1, replica_groups=mesh['mid'=2,'low'=2,'z'=4,'core'=2,'x'=4,'y'=4] {'low','z','core'}, dimensions={0} | all-to-all | bytes 262144 | tf_op jit(solution)/shard_map/all_to_all | solution.py:26
  252.9 0.1 select_convert_fusion.4
  253.0 9.8 %all_to_all.111 = bf16[16,16,256]{2,1,0:T(8,128)(2,1)S(1)} all-to-all(bf16[16,16,256]{2,1,0:T(8,128)(2,1)S(1)} %broadcast_in_dim.151), channel_id=1, replica_groups=mesh['mid'=2,'low'=2,'z'=4,'core'=2,'x'=4,'y'=4] {'x','y'}, dimensions={0} | all-to-all | bytes 262144 | tf_op jit(solution)/shard_map/all_to_all | solution.py:19
  262.8 0.2 convolution_convert_fusion.6
  263.0 18.1 %all_to_all.112 = bf16[16,16,256]{2,1,0:T(8,128)(2,1)S(1)} all-to-all(bf16[16,16,256]{2,1,0:T(8,128)(2,1)S(1)} %bitcast.161), channel_id=1, replica_groups=mesh['mid'=2,'low'=2,'z'=4,'core'=2,'x'=4,'y'=4] {'low','z','core'}, dimensions={0} | all-to-all | bytes 262144 | tf_op jit(solution)/shard_map/all_to_all | solution.py:26
  281.1 0.1 select_convert_fusion.3
  281.2 2.8 collective-permute-start.3
  284.0 5.6 %collective-permute-done.3 = bf16[16,256]{1,0:T(8,128)(2,1)S(1)} collective-permute-done((bf16[16,256]{1,0:T(8,128)(2,1)S(1)}, bf16[16,256]{1,0:T(8,128)(2,1)S(1)}, u32[]{:S(2)}, u32[]{:S(2)}) %collective-permute-start.3) | collective-permute-done | bytes 8224 | tf_op jit(solution)/shard_map/ppermute | solution.py:13
  289.6 0.1 select_bitcast_fusion.1
  289.8 10.6 %all_to_all.113 = bf16[16,2,16,256]{3,2,1,0:T(8,128)(2,1)S(1)} all-to-all(bf16[16,2,16,256]{3,2,1,0:T(8,128)(2,1)S(1)} %broadcast_in_dim.152), channel_id=1, replica_groups=mesh['mid'=2,'low'=2,'z'=4,'core'=2,'x'=4,'y'=4] {'x','y'}, dimensions={0} | all-to-all | bytes 524288 | tf_op jit(solution)/shard_map/all_to_all | solution.py:97
  300.4 0.2 convolution_convert_fusion.5
  300.6 11.0 %all_to_all.114 = bf16[8,32,256]{2,1,0:T(8,128)(2,1)S(1)} all-to-all(bf16[8,32,256]{2,1,0:T(8,128)(2,1)S(1)} %bitcast.152), channel_id=1, replica_groups=mesh['mid'=2,'low'=2,'z'=4,'core'=2,'x'=4,'y'=4] {'z','core'}, dimensions={0} | all-to-all | bytes 262144 | tf_op jit(solution)/shard_map/all_to_all | solution.py:26
  311.6 0.1 select_convert_fusion.1
  311.8 10.7 %all_to_all.115 = bf16[16,32,256]{2,1,0:T(8,128)(2,1)S(1)} all-to-all(bf16[16,32,256]{2,1,0:T(8,128)(2,1)S(1)} %broadcast_in_dim.153), channel_id=1, replica_groups=mesh['mid'=2,'low'=2,'z'=4,'core'=2,'x'=4,'y'=4] {'x','y'}, dimensions={0} | all-to-all | bytes 524288 | tf_op jit(solution)/shard_map/all_to_all | solution.py:19
  322.4 0.2 convolution_convert_fusion.4
  322.7 10.6 %all_to_all.116 = bf16[8,32,256]{2,1,0:T(8,128)(2,1)S(1)} all-to-all(bf16[8,32,256]{2,1,0:T(8,128)(2,1)S(1)} %bitcast.162), channel_id=1, replica_groups=mesh['mid'=2,'low'=2,'z'=4,'core'=2,'x'=4,'y'=4] {'z','core'}, dimensions={0} | all-to-all | bytes 262144 | tf_op jit(solution)/shard_map/all_to_all | solution.py:26
  333.3 0.1 select_convert_fusion
  333.3 1.2 fusion.2
  334.5 1.0 copy.27
  (58 shorter events, 0.7 us)
Async XLA Ops:
  0.6 2.2 copy-start
  2.8 1.8 copy-start.8
  2.8 1.8 copy-start.9
  2.9 17.3 %copy-start.1 = (bf16[8,1,32,512]{3,2,1,0:T(8,128)(2,1)S(1)}, bf16[8,1,32,512]{3,2,1,0:T(8,128)(2,1)}, u32[]{:S(2)}) copy-start(bf16[8,1,32,512]{3,2,1,0:T(8,128)(2,1)} %param.20) | copy-start | bytes 786436
  4.7 15.5 %copy-start.4 = (bf16[1024,256]{1,0:T(8,128)(2,1)}, bf16[1024,256]{1,0:T(8,128)(2,1)S(1)}, u32[]{:S(2)}) copy-start(bf16[1024,256]{1,0:T(8,128)(2,1)S(1)} %convolution_convert_fusion.1) | copy-start | bytes 1572868
  4.7 34.2 %copy-start.6 = (bf16[8,1,32,2,256]{4,3,2,1,0:T(2,128)(2,1)S(1)}, bf16[8,1,32,2,256]{4,3,2,1,0:T(2,128)(2,1)}, u32[]{:S(2)}) copy-start(bf16[8,1,32,2,256]{4,3,2,1,0:T(2,128)(2,1)} %param.22) | copy-start | bytes 786436
  20.5 46.2 %copy-start.11 = (bf16[16,256]{1,0:T(8,128)(2,1)S(1)}, bf16[16,256]{1,0:T(8,128)(2,1)}, u32[]{:S(2)}) copy-start(bf16[16,256]{1,0:T(8,128)(2,1)} %param.16) | copy-start | bytes 24580
  32.5 57.3 %copy-start.3 = (bf16[16,1,16,256]{3,2,1,0:T(8,128)(2,1)S(1)}, bf16[16,1,16,256]{3,2,1,0:T(8,128)(2,1)}, u32[]{:S(2)}) copy-start(bf16[16,1,16,256]{3,2,1,0:T(8,128)(2,1)} %param.19) | copy-start | bytes 393220
  33.3 11.4 %all-to-all-start.2 = ((bf16[8,32,256]{2,1,0:T(8,128)(2,1)}), bf16[8,32,256]{2,1,0:T(8,128)(2,1)S(1)}, u32[]{:S(2)}, u32[]{:S(2)}) async-start(bf16[8,32,256]{2,1,0:T(8,128)(2,1)} %broadcast_in_dim.142), calls=%async_computation.2 | async-start | bytes 262144 | tf_op jit(solution)/shard_map/all_to_all | solution.py:19
  44.7 73.5 %copy-start.2 = (bf16[16,1,16,2,128]{4,3,2,1,0:T(2,128)(2,1)S(1)}, bf16[16,1,16,2,128]{4,3,2,1,0:T(2,128)(2,1)}, u32[]{:S(2)}) copy-start(bf16[16,1,16,2,128]{4,3,2,1,0:T(2,128)(2,1)} %param.21) | copy-start | bytes 393220
  45.1 97.3 %copy-start.14 = (bf16[8,256]{1,0:T(8,128)(2,1)S(1)}, bf16[8,256]{1,0:T(8,128)(2,1)}, u32[]{:S(2)}) copy-start(bf16[8,256]{1,0:T(8,128)(2,1)} %param.15) | copy-start | bytes 12292
  45.8 122.7 %copy-start.7 = (bf16[32,1,8,128]{3,2,1,0:T(8,128)(2,1)S(1)}, bf16[32,1,8,128]{3,2,1,0:T(8,128)(2,1)}, u32[]{:S(2)}) copy-start(bf16[32,1,8,128]{3,2,1,0:T(8,128)(2,1)} %param.18) | copy-start | bytes 196612
  45.8 11.0 %all-to-all-start.3 = ((bf16[16,2,16,256]{3,2,1,0:T(8,128)(2,1)}), bf16[16,2,16,256]{3,2,1,0:T(8,128)(2,1)S(1)}, u32[]{:S(2)}, u32[]{:S(2)}) async-start(bf16[16,2,16,256]{3,2,1,0:T(8,128)(2,1)} %copy.22), calls=%async_computation.3 | async-start | bytes 524288 | tf_op jit(solution)/shard_map/all_to_all | solution.py:63
  56.9 9.9 %collective-permute-start = (bf16[16,256]{1,0:T(8,128)(2,1)S(1)}, bf16[16,256]{1,0:T(8,128)(2,1)S(1)}, u32[]{:S(2)}, u32[]{:S(2)}) collective-permute-start(bf16[16,256]{1,0:T(8,128)(2,1)S(1)} %fusion.22), channel_id=1, source_target_pairs={{0,128},{128,0},{1,129},{129,1},{2,130},{130,2},{3,131},{131,3},{4... | collective-permute-start | bytes 24584 | tf_op jit(solution)/shard_map/ppermute | solution.py:13
  119.1 10.2 %all-to-all-start.7 = ((bf16[16,2,8,256]{3,2,1,0:T(8,128)(2,1)}), bf16[16,2,8,256]{3,2,1,0:T(8,128)(2,1)S(1)}, u32[]{:S(2)}, u32[]{:S(2)}) async-start(bf16[16,2,8,256]{3,2,1,0:T(8,128)(2,1)} %bitcast.138), calls=%async_computation.7 | async-start | bytes 262144 | tf_op jit(solution)/shard_map/all_to_all | solution.py:63
  129.3 13.1 %collective-permute-start.1 = (bf16[8,256]{1,0:T(8,128)(2,1)S(1)}, bf16[8,256]{1,0:T(8,128)(2,1)S(1)}, u32[]{:S(2)}, u32[]{:S(2)}) collective-permute-start(bf16[8,256]{1,0:T(8,128)(2,1)S(1)} %fusion.26), channel_id=1, source_target_pairs={{0,256},{256,0},{1,257},{257,1},{2,258},{258,2},{3,259},{259,3},{4... | collective-permute-start | bytes 12296 | tf_op jit(solution)/shard_map/ppermute | solution.py:13
  211.5 89.1 %copy-start.13 = (bf16[8,256]{1,0:T(8,128)(2,1)}, bf16[8,256]{1,0:T(8,128)(2,1)S(1)}, u32[]{:S(2)}) copy-start(bf16[8,256]{1,0:T(8,128)(2,1)S(1)} %select_convert_fusion.7) | copy-start | bytes 12292
  211.5 13.1 %collective-permute-start.2 = (bf16[8,256]{1,0:T(8,128)(2,1)S(1)}, bf16[8,256]{1,0:T(8,128)(2,1)S(1)}, u32[]{:S(2)}, u32[]{:S(2)}) collective-permute-start(bf16[8,256]{1,0:T(8,128)(2,1)S(1)} %select_convert_fusion.7), channel_id=1, source_target_pairs={{0,256},{256,0},{1,257},{257,1},{2,258},{258,2},{3,259},{259,3},{4... | collective-permute-start | bytes 12296 | tf_op jit(solution)/shard_map/ppermute | solution.py:13
  281.2 52.0 %copy-start.12 = (bf16[16,256]{1,0:T(8,128)(2,1)}, bf16[16,256]{1,0:T(8,128)(2,1)S(1)}, u32[]{:S(2)}) copy-start(bf16[16,256]{1,0:T(8,128)(2,1)S(1)} %select_convert_fusion.3) | copy-start | bytes 24580
  281.2 8.4 %collective-permute-start.3 = (bf16[16,256]{1,0:T(8,128)(2,1)S(1)}, bf16[16,256]{1,0:T(8,128)(2,1)S(1)}, u32[]{:S(2)}, u32[]{:S(2)}) collective-permute-start(bf16[16,256]{1,0:T(8,128)(2,1)S(1)} %select_convert_fusion.3), channel_id=1, source_target_pairs={{0,128},{128,0},{1,129},{129,1},{2,130},{130,2},{3,131},{131,3},{4... | collective-permute-start | bytes 24584 | tf_op jit(solution)/shard_map/ppermute | solution.py:13
  289.8 43.6 %copy-start.5 = (bf16[1024,256]{1,0:T(8,128)(2,1)S(1)}, bf16[1024,256]{1,0:T(8,128)(2,1)}, u32[]{:S(2)}) copy-start(bf16[1024,256]{1,0:T(8,128)(2,1)} %copy-done.4) | copy-start | bytes 1572868
  333.3 2.2 copy-start.10

commit v2 on v1

v2 whole, which is shorter than its diff:
```python
import jax
import jax.numpy as jnp
from jax import lax
from jax.experimental import pallas as pl
from jax.experimental.pallas import tpu as pltpu
from jax.sharding import Mesh, PartitionSpec as P

FRONT = ("x", "y")
LEAF = ("mid", "low", "z", "core")
BLOCK = ("z", "core")
WAYS = 16
MEMBERS = 8
SLICE = 32
ROWS = 32
WIDTH = MEMBERS * SLICE
SMALL = (ROWS, WIDTH)
SENT = (WAYS, ROWS, WIDTH)
FRONT_AT, MID_AT, CORE_AT = 3, 4, 5
F32 = jnp.float32
BF16 = jnp.bfloat16


def swap(array, axis):
    return lax.ppermute(array, axis, [(0, 1), (1, 0)])


def exchange(blocks, axes):
    return lax.all_to_all(blocks, axes, 0, 0, tiled=True)


def gather(block, axes):
    ways = lax.axis_size(axes)
    return exchange(jnp.broadcast_to(block[None], (ways,) + block.shape), axes)


def after(array, chain):
    return array + jnp.minimum(jnp.abs(chain[:1, :1]), 0.0).astype(array.dtype)


def in_order(position, own, other, axis):
    return jnp.where(
        position == 0,
        jnp.concatenate([own, other], axis=axis),
        jnp.concatenate([other, own], axis=axis),
    )


def product_rows(gathered, matrix, piece, out_piece):
    columns = gathered.reshape(MEMBERS, ROWS // piece, piece, WIDTH)
    columns = columns.transpose(1, 0, 2, 3).reshape(MEMBERS * ROWS, WIDTH)
    product = lax.dot_general(
        matrix, columns, (((0,), (0,)), ((), ())), preferred_element_type=F32
    ).astype(BF16)
    product = product.reshape(ROWS // out_piece, WAYS, out_piece, WIDTH).transpose(1, 0, 2, 3)
    return jnp.sum(exchange(product.reshape(SENT), FRONT).astype(F32), axis=0)


def lane_group(rows):
    return lax.broadcasted_iota(jnp.int32, (rows, WIDTH), 1) // SLICE


def packed_mask(table_ref, level, piece):
    row = lax.broadcasted_iota(jnp.int32, SMALL, 0)
    member = row // piece * MEMBERS + lane_group(ROWS)
    index = (member * WAYS + table_ref[FRONT_AT]) * piece + row % piece
    return index < table_ref[level]


def source_rows(recv_ref, piece):
    parts = []
    for o in range(ROWS // piece):
        rows = recv_ref[:, o * piece : (o + 1) * piece, :].astype(F32)
        parts.append(rows.reshape(WAYS * piece, WIDTH))
    return jnp.concatenate(parts, axis=0).astype(BF16)


def apply_transposed(weights_ref, recv_ref, row_piece, piece):
    source = source_rows(recv_ref, row_piece)
    group = lane_group(WIDTH)
    total = jnp.zeros((WIDTH, WIDTH), F32)
    for m in range(MEMBERS):
        term = jnp.dot(weights_ref[m], source, preferred_element_type=F32)
        total = jnp.where(group == m, term, total)
    for step in (4 * SLICE, 2 * SLICE, SLICE):
        total = total + pltpu.roll(total, step, 1)
    group = lane_group(piece)
    packed = []
    for o in range(ROWS // piece):
        rows = jnp.zeros((piece, WIDTH), F32)
        for m in range(MEMBERS):
            start = (o * MEMBERS + m) * piece
            rows = jnp.where(group == m, total[start : start + piece], rows)
        packed.append(rows)
    return jnp.concatenate(packed, axis=0)


def whole(shape):
    return pl.BlockSpec(shape, lambda i: (0,) * len(shape))


def call(body, table, operands, specs, shapes):
    return pl.pallas_call(
        body,
        grid=(1,),
        in_specs=[pl.BlockSpec(memory_space=pltpu.SMEM)] + specs,
        out_specs=[whole(shape) for shape in shapes],
        out_shape=[jax.ShapeDtypeStruct(shape, BF16) for shape in shapes],
        compiler_params=pltpu.CompilerParams(vmem_limit_bytes=32 << 20),
    )(table, *operands)


def weight_spec(part):
    return pl.BlockSpec((MEMBERS, WIDTH, 2 * WIDTH), lambda i: (0, 0, part))


def backward_solve(table, level, recv, weights, piece):
    def body(table_ref, recv_ref, weights_ref, solved_ref, send_ref):
        value = apply_transposed(weights_ref, recv_ref, piece, piece)
        solved = jnp.where(packed_mask(table_ref, level, piece), value, 0.0).astype(BF16)
        solved_ref[...] = solved
        send_ref[...] = jnp.broadcast_to(solved[None], SENT)

    return call(body, table, (recv, weights), [whole(SENT), weight_spec(0)], [SMALL, SENT])


def backward_residual(table, level, recv, forward, weights, row_piece, piece):
    def body(table_ref, recv_ref, forward_ref, weights_ref, send_ref):
        value = forward_ref[...].astype(F32)
        value = value - apply_transposed(weights_ref, recv_ref, row_piece, piece)
        residual = jnp.where(packed_mask(table_ref, level, piece), value, 0.0).astype(BF16)
        send_ref[...] = jnp.broadcast_to(residual[None], SENT)

    return call(
        body,
        table,
        (recv, forward, weights),
        [whole(SENT), whole(SMALL), weight_spec(1)],
        [SENT],
    )[0]


def order_shares(table, shares, chain):
    def body(table_ref, shares_ref, chain_ref, middle_ref, matrix_ref, update_ref, root_ref):
        core = table_ref[CORE_AT]
        for o in range(2):
            block = shares_ref[table_ref[MID_AT] * 4 + o * 2 + core, :, :WIDTH]
            matrix_ref[:, o * WIDTH : (o + 1) * WIDTH] = block
            middle_ref[:, o * WIDTH : (o + 1) * WIDTH] = block
            for h in range(2):
                block = shares_ref[table_ref[MID_AT] * 4 + o * 2 + core, :, WIDTH + h * 128 : WIDTH + h * 128 + 128]
                start = (h * 2 + o) * 128
                update_ref[:, start : start + 128] = block
                middle_ref[:, 2 * WIDTH + start : 2 * WIDTH + start + 128] = block
        for o in range(4):
            root_ref[:, o * 128 : o * 128 + 128] = shares_ref[o * 2 + core, :, 2 * WIDTH :]

    pair = (WIDTH, 2 * WIDTH)
    return call(
        body,
        table,
        (shares, chain),
        [whole(shares.shape), pl.BlockSpec(memory_space=pl.ANY)],
        [(WIDTH, 4 * WIDTH), pair, pair, pair],
    )


SPLIT = (MEMBERS, ROWS + 8, WIDTH)


def root_transposed(table, recv, matrix, kept, piece):
    def body(table_ref, recv_ref, matrix_ref, kept_ref, send_ref):
        product = jnp.dot(
            matrix_ref[...], source_rows(recv_ref, piece), preferred_element_type=F32
        )
        kept_rows = kept_ref[...].astype(F32)
        turned = [product] + [pltpu.roll(product, SLICE * d, 1) for d in range(1, MEMBERS)]
        kept_turned = [kept_rows] + [pltpu.roll(kept_rows, SLICE * d, 1) for d in range(1, MEMBERS)]
        group = lane_group(8)
        for target in range(MEMBERS):
            blocks = []
            for o in range(ROWS // piece):
                rows = jnp.zeros((piece, WIDTH), F32)
                for m in range(MEMBERS):
                    start = (o * MEMBERS + m) * piece
                    moved = turned[(m - target) % MEMBERS][start : start + piece]
                    rows = jnp.where(group == m, moved, rows)
                blocks.append(rows)
            rows = jnp.zeros((8, WIDTH), F32)
            for q in range(8):
                moved = kept_turned[(q - target) % MEMBERS][q * 8 : q * 8 + 8]
                rows = jnp.where(group == q, moved, rows)
            blocks.append(rows)
            send_ref[target] = jnp.concatenate(blocks, axis=0).astype(BF16)

    return call(
        body,
        table,
        (recv, matrix, kept),
        [whole(SENT), whole((WIDTH, 2 * WIDTH)), whole((2 * ROWS, WIDTH))],
        [SPLIT],
    )[0]


def root_collect(table, level, recv, piece):
    def body(table_ref, recv_ref, solved_ref, mid_ref, low_ref, send_ref):
        blocks = [recv_ref[m].astype(F32) for m in range(MEMBERS)]
        total = blocks[0][:ROWS]
        for m in range(1, MEMBERS):
            total = total + blocks[m][:ROWS]
        solved = jnp.where(packed_mask(table_ref, level, piece), total, 0.0).astype(BF16)
        solved_ref[...] = solved
        send_ref[...] = jnp.broadcast_to(solved[None], SENT)
        group = lane_group(8)
        kept = []
        for q in range(8):
            rows = jnp.zeros((8, WIDTH), F32)
            for m in range(MEMBERS):
                moved = blocks[m][ROWS:]
                shift = (m - q) % MEMBERS
                if shift:
                    moved = pltpu.roll(moved, SLICE * shift, 1)
                rows = jnp.where(group == m, moved, rows)
            kept.append(rows)
        mid_ref[...] = jnp.concatenate(kept[:4], axis=0).astype(BF16)
        low_ref[...] = jnp.concatenate(kept[4:], axis=0).astype(BF16)

    return call(body, table, (recv,), [whole(SPLIT)], [SMALL, SMALL, SMALL, SENT])


def from_slices(rows):
    count = rows.shape[0]
    sent = rows.reshape(count, MEMBERS, SLICE).transpose(1, 0, 2)
    return exchange(sent, BLOCK).transpose(1, 0, 2).reshape(count, WIDTH)


def shards(
    subtree_rhs,
    subtree_inverse,
    coupling,
    rhs_top,
    rhs_mid,
    rhs_low,
    inverse_top,
    inverse_mid,
    inverse_low,
    update_mid,
    update_low,
    front_rows,
):
    mid_pos = lax.axis_index("mid")
    low_pos = lax.axis_index("low")
    front_pos = lax.axis_index(FRONT)
    member = lax.axis_index(BLOCK)
    piece_top, piece_mid, piece_low = rhs_top.shape[0], rhs_mid.shape[0], rhs_low.shape[0]
    low_matrix = inverse_low.reshape(WIDTH, -1)
    low_update = update_low.reshape(WIDTH, -1)

    lookup = jnp.arange(front_rows.shape[0], dtype=jnp.int32)

    def live(index):
        return jnp.sum(jnp.where(lookup == index, front_rows, 0))

    def row_mask(live_rows, piece):
        row = jnp.arange(ROWS, dtype=jnp.int32)
        place = (row // piece * MEMBERS + member) * WAYS + front_pos
        return (place * piece + row % piece < live_rows)[:, None]

    live_top, live_mid, live_low = live(0), live(1 + mid_pos), live(3 + mid_pos * 2 + low_pos)
    table = jnp.stack(
        [live_top, live_mid, live_low, front_pos, mid_pos, lax.axis_index("core")]
    ).astype(jnp.int32)
    mask_top = row_mask(live_top, piece_top)
    mask_mid = row_mask(live_mid, piece_mid)
    mask_low = row_mask(live_low, piece_low)

    def rounded(mask, value):
        return jnp.where(mask, value, 0.0).astype(BF16)

    below_solved = jnp.dot(subtree_inverse, subtree_rhs, preferred_element_type=F32).astype(BF16)
    pushed = jnp.dot(coupling, below_solved, preferred_element_type=F32)
    right_low = rounded(mask_low, rhs_low.astype(F32) - pushed)
    columns = gather(right_low, BLOCK)
    own = jnp.concatenate(
        [
            inverse_mid.reshape(WIDTH, -1),
            update_mid.reshape(WIDTH, -1),
            inverse_top.reshape(WIDTH, -1),
        ],
        axis=1,
    )
    shares = lax.all_gather(own, ("mid", "low", "core"), axis=0, tiled=False)
    forward_low = rounded(mask_low, product_rows(columns, low_matrix, piece_low, piece_low))

    lifted = product_rows(gather(forward_low, BLOCK), low_update, piece_low, piece_mid)
    half = jnp.arange(2, dtype=jnp.int32)[:, None, None]
    share = jnp.where(half == low_pos, rhs_mid.astype(F32)[None], 0.0)
    share = (share.reshape(SMALL) - lifted).astype(BF16)
    shared = swap(jnp.concatenate([share, rhs_top], axis=0), "low")
    right_mid = rounded(mask_mid, share.astype(F32) + shared[:ROWS].astype(F32))
    rhs_pair = in_order(low_pos, rhs_top, shared[ROWS:], 0)

    columns = gather(right_mid, BLOCK)
    middle, mid_matrix, mid_update, top_matrix = order_shares(table, shares, right_mid)
    middle = lax.all_gather(middle, BLOCK, axis=0, tiled=False)
    forward_mid = rounded(mask_mid, product_rows(columns, mid_matrix, piece_mid, piece_mid))

    low = after(jnp.concatenate([low_matrix, low_update], axis=1), forward_mid)
    low = lax.all_gather(low, BLOCK, axis=0, tiled=False)

    lifted = product_rows(gather(forward_mid, BLOCK), mid_update, piece_mid, piece_top)
    share = jnp.where(half == mid_pos, rhs_pair.astype(F32)[None], 0.0)
    share = (share.reshape(SMALL) - lifted).astype(BF16)
    right_top = rounded(mask_top, share.astype(F32) + swap(share, "mid").astype(F32))

    columns = gather(right_top, BLOCK)
    forward_top = rounded(mask_top, product_rows(columns, top_matrix, piece_top, piece_top))
    kept = jnp.concatenate([forward_mid, forward_low], axis=0)
    sent = root_transposed(table, gather(forward_top, FRONT), top_matrix, kept, piece_top)
    solution_top, forward_mid, forward_low, sent = root_collect(
        table, 0, exchange(sent, BLOCK), piece_top
    )
    sent = backward_residual(
        table, 1, exchange(sent, FRONT), forward_mid, middle, piece_top, piece_mid
    )
    solution_mid, sent = backward_solve(table, 1, exchange(sent, FRONT), middle, piece_mid)
    sent = backward_residual(
        table, 2, exchange(sent, FRONT), forward_low, low, piece_mid, piece_low
    )
    solution_low, _ = backward_solve(table, 2, exchange(sent, FRONT), low, piece_low)

    own_mid = lax.dynamic_slice_in_dim(solution_mid, low_pos * piece_mid, piece_mid, 0)
    own_top = lax.dynamic_slice_in_dim(
        solution_top, (mid_pos * 2 + low_pos) * piece_top, piece_top, 0
    )
    solved = from_slices(jnp.concatenate([solution_low, own_mid, own_top], axis=0))
    solution_low = solved[:piece_low]
    solution_mid = solved[piece_low : piece_low + piece_mid]
    solution_top = solved[piece_low + piece_mid :]

    moved = lax.dot_general(
        coupling, solution_low, (((0,), (0,)), ((), ())), preferred_element_type=F32
    )
    shifted = (below_solved.astype(F32) - moved).astype(BF16)
    solution_sub = lax.dot_general(
        subtree_inverse, shifted, (((0,), (0,)), ((), ())), preferred_element_type=F32
    ).astype(BF16)
    return (solution_sub, solution_top, solution_mid, solution_low)


def solution(mesh):
    fine = Mesh(mesh.devices.reshape(2, 2, 4, 2, 4, 4), LEAF + FRONT)
    rows = P(LEAF + FRONT, None)
    placed = (rows,) * 6 + (
        P(None, FRONT, None, LEAF),
        P(None, FRONT, None, LEAF),
        P(None, FRONT, None, LEAF),
        P(None, FRONT, None, None, LEAF),
        P(None, FRONT, None, None, LEAF),
        P(),
    )
    return jax.shard_map(
        shards, mesh=fine, in_specs=placed, out_specs=(rows, rows, rows, rows), check_vma=False
    )
```

time: 337 us -> 301 us (0.89)
  blocking collectives: 245 us -> 127 us
  waiting for transfers between devices: 40.5 us -> 66.1 us
  local copies, waits for them, and re-layouts: 3.56 us -> 20.9 us
  between operations: 1.11 us -> 14.9 us
  starting transfers between devices: 35.1 us -> 47.3 us
  Pallas kernels: 0 us -> 10.7 us
    all_to_all x17 -> x10, blocking collectives: 245 us -> 127 us  [exchange(): return lax.all_to_all(blocks, axes, 0, 0, tiled=True)]
    all_to_all x3 -> x7, waiting for transfers between devices: 19.8 us -> 65.2 us  [exchange(): return lax.all_to_all(blocks, axes, 0, 0, tiled=True)]
    ppermute x4 -> x2, waiting for transfers between devices: 20.7 us -> 0.84 us  [swap(): return lax.ppermute(array, axis, [(0, 1), (1, 0)])]
    all_to_all x3 -> x7, starting transfers between devices: 12.7 us -> 26.8 us  [exchange(): return lax.all_to_all(blocks, axes, 0, 0, tiled=True)]
    unnamed x32 -> x36, local copies, waits for them, and re-layouts: 1.11 us -> 12.8 us
    pallas_call x0 -> x7, Pallas kernels: none -> 10.7 us  [call(): pl.pallas_call(body, grid=(1,), in_specs=[pl.BlockSpec(memory_space=pltpu...]
    ppermute x4 -> x2, starting transfers between devices: 22.3 us -> 20.4 us  [swap(): return lax.ppermute(array, axis, [(0, 1), (1, 0)])]
  transfers between devices with their start and end apart: 7 -> 12, of which waited for: 7 -> 8; matrix products, arithmetic and copies ran while one was open for 0% -> 6% of each run, Pallas kernels for 0% -> 2%
where the time goes in v2:
time: 301 us; the launch traced here: 299 us
  blocking collectives  127 us (42%)
  waiting for transfers between devices  66.1 us (22%)
  starting transfers between devices  47.3 us (16%)
  local copies, waits for them, and re-layouts  20.9 us (7%)
  between operations  14.9 us (5%)
  Pallas kernels  10.7 us (4%)
  other arithmetic  7.77 us (3%)
  matrix products  4.44 us (1%)
    all_to_all x10, blocking collectives, exchange(): return lax.all_to_all(blocks, axes, 0, 0, tiled=True)  127 us
    all_to_all x7, waiting for transfers between devices, exchange(): return lax.all_to_all(blocks, axes, 0, 0, tiled=True)  65.2 us
    all_to_all x7, starting transfers between devices, exchange(): return lax.all_to_all(blocks, axes, 0, 0, tiled=True)  26.8 us
    ppermute x2, starting transfers between devices, swap(): return lax.ppermute(array, axis, [(0, 1), (1, 0)])  20.4 us
    unnamed x36, local copies, waits for them, and re-layouts  12.8 us
    pallas_call x7, Pallas kernels, call(): pl.pallas_call(body, grid=(1,), in_specs=[pl.BlockSpec(memory_space=pltpu...  10.7 us
  transfers between devices with their start and end apart: 12, of which 8 were waited for; matrix products, arithmetic and copies ran while one was open for 6% of the time, Pallas kernels for 2%

profile of v2, /device:TPU:1, one launch (start us, length us, event | category | flops | bytes accessed | tf_op | source)
XLA Modules:
  0.0 299.2 jit_solution(18259902308278552751)
XLA Ops:
  7.2 1.1 copy.66
  8.3 1.7 pad_maximum_fusion
  10.0 1.4 fusion.23
  11.4 0.7 fusion.17
  12.1 1.8 convolution_convert_fusion.1
  14.2 15.2 %all_to_all.85 = bf16[8,32,256]{2,1,0:T(8,128)(2,1)S(1)} all-to-all(bf16[8,32,256]{2,1,0:T(8,128)(2,1)S(1)} %broadcast_in_dim.132), channel_id=1, replica_groups=mesh['mid'=2,'low'=2,'z'=4,'core'=2,'x'=4,'y'=4] {'z','core'}, dimensions={0} | all-to-all | bytes 262144 | tf_op jit(solution)/shard_map/all_to_all | solution.py:28
  29.4 0.2 fusion.3
  29.8 12.0 %all_to_all.86 = bf16[16,32,256]{2,1,0:T(8,128)(2,1)S(1)} all-to-all(bf16[16,32,256]{2,1,0:T(8,128)(2,1)S(1)} %bitcast.126), channel_id=1, replica_groups=mesh['mid'=2,'low'=2,'z'=4,'core'=2,'x'=4,'y'=4] {'x','y'}, dimensions={0} | all-to-all | bytes 524288 | tf_op jit(solution)/shard_map/all_to_all | solution.py:28
  42.0 0.7 broadcast_in_dim.133
  42.6 5.5 %all-to-all-start.2 = ((bf16[8,32,256]{2,1,0:T(8,128)(2,1)}), bf16[8,32,256]{2,1,0:T(8,128)(2,1)S(1)}, u32[]{:S(2)}, u32[]{:S(2)}) async-start(bf16[8,32,256]{2,1,0:T(8,128)(2,1)} %broadcast_in_dim.133), calls=%async_computation.2 | async-start | bytes 262144 | tf_op jit(solution)/shard_map/all_to_all | solution.py:28
  48.2 22.6 %all-to-all-done.2 = bf16[8,32,256]{2,1,0:T(8,128)(2,1)S(1)} async-done(((bf16[8,32,256]{2,1,0:T(8,128)(2,1)}), bf16[8,32,256]{2,1,0:T(8,128)(2,1)S(1)}, u32[]{:S(2)}, u32[]{:S(2)}) %all-to-all-start.2) | async-done | bytes 131104 | tf_op jit(solution)/shard_map/all_to_all | solution.py:28
  70.8 0.2 fusion.4
  71.2 0.8 copy.45
  71.9 3.5 %all-to-all-start.3 = ((bf16[16,32,256]{2,1,0:T(8,128)(2,1)}), bf16[16,32,256]{2,1,0:T(8,128)(2,1)S(1)}, u32[]{:S(2)}, u32[]{:S(2)}) async-start(bf16[16,32,256]{2,1,0:T(8,128)(2,1)} %bitcast.19), calls=%async_computation.3 | async-start | bytes 524288 | tf_op jit(solution)/shard_map/all_to_all | solution.py:28
  75.7 7.2 %all-to-all-done.3 = bf16[16,32,256]{2,1,0:T(8,128)(2,1)S(1)} async-done(((bf16[16,32,256]{2,1,0:T(8,128)(2,1)}), bf16[16,32,256]{2,1,0:T(8,128)(2,1)S(1)}, u32[]{:S(2)}, u32[]{:S(2)}) %all-to-all-start.3) | async-done | bytes 262176 | tf_op jit(solution)/shard_map/all_to_all | solution.py:28
  83.1 6.1 %collective-permute-start = (bf16[40,256]{1,0:T(8,128)(2,1)S(1)}, bf16[40,256]{1,0:T(8,128)(2,1)S(1)}, u32[]{:S(2)}, u32[]{:S(2)}) collective-permute-start(bf16[40,256]{1,0:T(8,128)(2,1)S(1)} %pad_maximum_fusion.3), channel_id=1, source_target_pairs={{0,128},{128,0},{1,129},{129,1},{2,130},{130,2},{3,131},{131,3},{4... | collective-permute-start | bytes 61448 | tf_op jit(solution)/shard_map/ppermute | solution.py:24
  89.2 0.7 fusion.18
  89.9 2.1 stack.27.table_ref
  92.0 1.7 copy-done.5
  93.7 1.5 shard_map.147
  95.3 14.5 %all_to_all.87 = bf16[8,32,256]{2,1,0:T(8,128)(2,1)S(1)} all-to-all(bf16[8,32,256]{2,1,0:T(8,128)(2,1)S(1)} %broadcast_in_dim.139), channel_id=1, replica_groups=mesh['mid'=2,'low'=2,'z'=4,'core'=2,'x'=4,'y'=4] {'z','core'}, dimensions={0} | all-to-all | bytes 262144 | tf_op jit(solution)/shard_map/all_to_all | solution.py:28
  109.8 0.3 convolution_convert_fusion.4
  110.1 0.7 copy.47
  110.8 3.5 %all-to-all-start.5 = ((bf16[16,32,256]{2,1,0:T(8,128)(2,1)}), bf16[16,32,256]{2,1,0:T(8,128)(2,1)S(1)}, u32[]{:S(2)}, u32[]{:S(2)}) async-start(bf16[16,32,256]{2,1,0:T(8,128)(2,1)} %bitcast.26), calls=%async_computation.5 | async-start | bytes 524288 | tf_op jit(solution)/shard_map/all_to_all | solution.py:28
  114.4 0.9 concatenate.46
  115.3 6.4 %all-to-all-done.5 = bf16[16,32,256]{2,1,0:T(8,128)(2,1)S(1)} async-done(((bf16[16,32,256]{2,1,0:T(8,128)(2,1)}), bf16[16,32,256]{2,1,0:T(8,128)(2,1)S(1)}, u32[]{:S(2)}, u32[]{:S(2)}) %all-to-all-start.5) | async-done | bytes 262176 | tf_op jit(solution)/shard_map/all_to_all | solution.py:28
  121.8 0.5 slice.38
  123.0 1.9 maximum_add_fusion
  124.9 12.6 %all_to_all.88 = bf16[8,32,256]{2,1,0:T(8,128)(2,1)S(1)} all-to-all(bf16[8,32,256]{2,1,0:T(8,128)(2,1)S(1)} %broadcast_in_dim.140), channel_id=1, replica_groups=mesh['mid'=2,'low'=2,'z'=4,'core'=2,'x'=4,'y'=4] {'z','core'}, dimensions={0} | all-to-all | bytes 262144 | tf_op jit(solution)/shard_map/all_to_all | solution.py:28
  137.5 0.3 convolution_convert_fusion.3
  137.8 0.7 copy.65
  138.5 3.5 %all-to-all-start.7 = ((bf16[16,32,256]{2,1,0:T(8,128)(2,1)}), bf16[16,32,256]{2,1,0:T(8,128)(2,1)S(1)}, u32[]{:S(2)}, u32[]{:S(2)}) async-start(bf16[16,32,256]{2,1,0:T(8,128)(2,1)} %bitcast.116), calls=%async_computation.7 | async-start | bytes 524288 | tf_op jit(solution)/shard_map/all_to_all | solution.py:28
  142.2 7.1 %all-to-all-done.7 = bf16[16,32,256]{2,1,0:T(8,128)(2,1)S(1)} async-done(((bf16[16,32,256]{2,1,0:T(8,128)(2,1)}), bf16[16,32,256]{2,1,0:T(8,128)(2,1)S(1)}, u32[]{:S(2)}, u32[]{:S(2)}) %all-to-all-start.7) | async-done | bytes 262176 | tf_op jit(solution)/shard_map/all_to_all | solution.py:28
  149.5 14.3 %collective-permute-start.1 = (bf16[32,256]{1,0:T(8,128)(2,1)S(1)}, bf16[32,256]{1,0:T(8,128)(2,1)S(1)}, u32[]{:S(2)}, u32[]{:S(2)}) collective-permute-start(bf16[32,256]{1,0:T(8,128)(2,1)S(1)} %fusion.10), channel_id=1, source_target_pairs={{0,256},{256,0},{1,257},{257,1},{2,258},{258,2},{3,259},{259,3},{4... | collective-permute-start | bytes 49160 | tf_op jit(solution)/shard_map/ppermute | solution.py:24
  163.8 0.7 fusion.19
  164.4 0.8 collective-permute-done.1
  165.4 11.8 %all_to_all.89 = bf16[8,32,256]{2,1,0:T(8,128)(2,1)S(1)} all-to-all(bf16[8,32,256]{2,1,0:T(8,128)(2,1)S(1)} %broadcast_in_dim.141), channel_id=1, replica_groups=mesh['mid'=2,'low'=2,'z'=4,'core'=2,'x'=4,'y'=4] {'z','core'}, dimensions={0} | all-to-all | bytes 262144 | tf_op jit(solution)/shard_map/all_to_all | solution.py:28
  177.2 0.3 convolution_convert_fusion.2
  177.5 10.8 %all_to_all.90 = bf16[16,32,256]{2,1,0:T(8,128)(2,1)S(1)} all-to-all(bf16[16,32,256]{2,1,0:T(8,128)(2,1)S(1)} %bitcast.129), channel_id=1, replica_groups=mesh['mid'=2,'low'=2,'z'=4,'core'=2,'x'=4,'y'=4] {'x','y'}, dimensions={0} | all-to-all | bytes 524288 | tf_op jit(solution)/shard_map/all_to_all | solution.py:28
  188.4 0.7 broadcast_in_dim.142
  189.2 3.6 %all-to-all-start.10 = ((bf16[16,32,256]{2,1,0:T(8,128)(2,1)}), bf16[16,32,256]{2,1,0:T(8,128)(2,1)S(1)}, u32[]{:S(2)}, u32[]{:S(2)}) async-start(bf16[16,32,256]{2,1,0:T(8,128)(2,1)} %broadcast_in_dim.142), calls=%async_computation.10 | async-start | bytes 524288 | tf_op jit(solution)/shard_map/all_to_all | solution.py:28
  192.8 7.4 %all-to-all-done.10.recv_ref = bf16[16,32,256]{2,1,0:T(8,128)(2,1)S(1)} async-done(((bf16[16,32,256]{2,1,0:T(8,128)(2,1)}), bf16[16,32,256]{2,1,0:T(8,128)(2,1)S(1)}, u32[]{:S(2)}, u32[]{:S(2)}) %all-to-all-start.10) | async-done | bytes 262176 | tf_op jit(solution)/shard_map/all_to_all | solution.py:28
  200.2 0.9 shard_map.148
  201.1 15.1 %all_to_all.91.recv_ref = bf16[8,40,256]{2,1,0:T(8,128)(2,1)S(1)} all-to-all(bf16[8,40,256]{2,1,0:T(8,128)(2,1)S(1)} %shard_map.148), channel_id=1, replica_groups=mesh['mid'=2,'low'=2,'z'=4,'core'=2,'x'=4,'y'=4] {'z','core'}, dimensions={0} | all-to-all | bytes 327680 | tf_op jit(solution)/shard_map/all_to_all | solution.py:28
  216.2 0.6 shard_map.149
  216.8 10.5 %all_to_all.92.recv_ref = bf16[16,32,256]{2,1,0:T(8,128)(2,1)S(1)} all-to-all(bf16[16,32,256]{2,1,0:T(8,128)(2,1)S(1)} %get-tuple-element.18), channel_id=1, replica_groups=mesh['mid'=2,'low'=2,'z'=4,'core'=2,'x'=4,'y'=4] {'x','y'}, dimensions={0} | all-to-all | bytes 524288 | tf_op jit(solution)/shard_map/all_to_all | solution.py:28
  227.3 2.2 copy-done.3
  229.5 1.4 shard_map.150
  230.9 11.1 %all_to_all.93.recv_ref = bf16[16,32,256]{2,1,0:T(8,128)(2,1)S(1)} all-to-all(bf16[16,32,256]{2,1,0:T(8,128)(2,1)S(1)} %shard_map.150), channel_id=1, replica_groups=mesh['mid'=2,'low'=2,'z'=4,'core'=2,'x'=4,'y'=4] {'x','y'}, dimensions={0} | all-to-all | bytes 524288 | tf_op jit(solution)/shard_map/all_to_all | solution.py:28
  242.0 2.1 shard_map.151
  244.1 3.5 %all-to-all-start.14 = ((bf16[16,32,256]{2,1,0:T(8,128)(2,1)}), bf16[16,32,256]{2,1,0:T(8,128)(2,1)S(1)}, u32[]{:S(2)}, u32[]{:S(2)}) async-start(bf16[16,32,256]{2,1,0:T(8,128)(2,1)} %get-tuple-element.21), calls=%async_computation.14 | async-start | bytes 524288 | tf_op jit(solution)/shard_map/all_to_all | solution.py:28
  247.7 7.3 %all-to-all-done.14.recv_ref = bf16[16,32,256]{2,1,0:T(8,128)(2,1)S(1)} async-done(((bf16[16,32,256]{2,1,0:T(8,128)(2,1)}), bf16[16,32,256]{2,1,0:T(8,128)(2,1)S(1)}, u32[]{:S(2)}, u32[]{:S(2)}) %all-to-all-start.14) | async-done | bytes 262176 | tf_op jit(solution)/shard_map/all_to_all | solution.py:28
  255.0 2.2 copy-done.1
  257.2 2.1 shard_map.152
  259.3 3.5 %all-to-all-start.15 = ((bf16[16,32,256]{2,1,0:T(8,128)(2,1)}), bf16[16,32,256]{2,1,0:T(8,128)(2,1)S(1)}, u32[]{:S(2)}, u32[]{:S(2)}) async-start(bf16[16,32,256]{2,1,0:T(8,128)(2,1)} %shard_map.152), calls=%async_computation.15 | async-start | bytes 524288 | tf_op jit(solution)/shard_map/all_to_all | solution.py:28
  262.9 7.3 %all-to-all-done.15.recv_ref = bf16[16,32,256]{2,1,0:T(8,128)(2,1)S(1)} async-done(((bf16[16,32,256]{2,1,0:T(8,128)(2,1)}), bf16[16,32,256]{2,1,0:T(8,128)(2,1)S(1)}, u32[]{:S(2)}, u32[]{:S(2)}) %all-to-all-start.15) | async-done | bytes 262176 | tf_op jit(solution)/shard_map/all_to_all | solution.py:28
  270.1 2.2 copy-done.2
  272.3 2.1 shard_map.153
  274.7 13.4 %all_to_all.94 = bf16[8,2,896]{2,1,0:T(2,128)(2,1)S(1)} all-to-all(bf16[8,2,896]{2,1,0:T(2,128)(2,1)S(1)} %reshape.302), channel_id=1, replica_groups=mesh['mid'=2,'low'=2,'z'=4,'core'=2,'x'=4,'y'=4] {'z','core'}, dimensions={0} | all-to-all | bytes 57344 | tf_op jit(solution)/shard_map/all_to_all | solution.py:28
  288.5 1.2 fusion.2
  289.7 0.7 copy.57
  290.4 1.0 copy.54
  291.4 0.7 copy.55
  292.0 0.7 copy.56
  (78 shorter events, 2.5 us)
Async XLA Ops:
  7.2 4.9 %copy-start = (bf16[1024,1024]{1,0:T(8,128)(2,1)S(1)}, bf16[1024,1024]{1,0:T(8,128)(2,1)}, u32[]{:S(2)}) copy-start(bf16[1024,1024]{1,0:T(8,128)(2,1)} %param.13) | copy-start | bytes 6291460
  7.2 84.8 %all-gather.8.cloned.1.call-start = ((), (), s32[]{:S(2)}) async-start(), calls=%async_computation.18 | async-start | bytes 2949120 | tf_op jit(solution)/shard_map/all_gather | solution.py:291
  12.1 1.8 copy-start.10
  12.1 1.8 copy-start.11
  12.1 17.3 %copy-start.7 = (bf16[8,1,32,512]{3,2,1,0:T(8,128)(2,1)S(1)}, bf16[8,1,32,512]{3,2,1,0:T(8,128)(2,1)}, u32[]{:S(2)}) copy-start(bf16[8,1,32,512]{3,2,1,0:T(8,128)(2,1)} %param.20) | copy-start | bytes 786436
  14.0 15.5 %copy-start.8 = (bf16[1024,256]{1,0:T(8,128)(2,1)}, bf16[1024,256]{1,0:T(8,128)(2,1)S(1)}, u32[]{:S(2)}) copy-start(bf16[1024,256]{1,0:T(8,128)(2,1)S(1)} %convolution_convert_fusion.1) | copy-start | bytes 1572868
  14.0 34.2 %copy-start.6 = (bf16[8,1,32,2,256]{4,3,2,1,0:T(2,128)(2,1)S(1)}, bf16[8,1,32,2,256]{4,3,2,1,0:T(2,128)(2,1)}, u32[]{:S(2)}) copy-start(bf16[8,1,32,2,256]{4,3,2,1,0:T(2,128)(2,1)} %param.22) | copy-start | bytes 786436
  29.8 45.7 %copy-start.13 = (bf16[16,256]{1,0:T(8,128)(2,1)S(1)}, bf16[16,256]{1,0:T(8,128)(2,1)}, u32[]{:S(2)}) copy-start(bf16[16,256]{1,0:T(8,128)(2,1)} %param.16) | copy-start | bytes 24580
  29.8 53.2 %copy-start.12 = (bf16[8,256]{1,0:T(8,128)(2,1)S(1)}, bf16[8,256]{1,0:T(8,128)(2,1)}, u32[]{:S(2)}) copy-start(bf16[8,256]{1,0:T(8,128)(2,1)} %param.15) | copy-start | bytes 12292
  42.6 28.1 %all-to-all-start.2 = ((bf16[8,32,256]{2,1,0:T(8,128)(2,1)}), bf16[8,32,256]{2,1,0:T(8,128)(2,1)S(1)}, u32[]{:S(2)}, u32[]{:S(2)}) async-start(bf16[8,32,256]{2,1,0:T(8,128)(2,1)} %broadcast_in_dim.133), calls=%async_computation.2 | async-start | bytes 262144 | tf_op jit(solution)/shard_map/all_to_all | solution.py:28
  71.9 11.0 %all-to-all-start.3 = ((bf16[16,32,256]{2,1,0:T(8,128)(2,1)}), bf16[16,32,256]{2,1,0:T(8,128)(2,1)S(1)}, u32[]{:S(2)}, u32[]{:S(2)}) async-start(bf16[16,32,256]{2,1,0:T(8,128)(2,1)} %bitcast.19), calls=%async_computation.3 | async-start | bytes 524288 | tf_op jit(solution)/shard_map/all_to_all | solution.py:28
  75.5 151.9 %all-gather.10.cloned.1.call-start = ((), (), s32[]{:S(2)}) async-start(), calls=%async_computation.19 | async-start | bytes 4718592 | tf_op jit(solution)/shard_map/all_gather | solution.py:304
  83.1 8.8 %collective-permute-start = (bf16[40,256]{1,0:T(8,128)(2,1)S(1)}, bf16[40,256]{1,0:T(8,128)(2,1)S(1)}, u32[]{:S(2)}, u32[]{:S(2)}) collective-permute-start(bf16[40,256]{1,0:T(8,128)(2,1)S(1)} %pad_maximum_fusion.3), channel_id=1, source_target_pairs={{0,128},{128,0},{1,129},{129,1},{2,130},{130,2},{3,131},{131,3},{4... | collective-permute-start | bytes 61448 | tf_op jit(solution)/shard_map/ppermute | solution.py:24
  92.0 1.7 copy-start.5
  110.8 10.9 %all-to-all-start.5 = ((bf16[16,32,256]{2,1,0:T(8,128)(2,1)}), bf16[16,32,256]{2,1,0:T(8,128)(2,1)S(1)}, u32[]{:S(2)}, u32[]{:S(2)}) async-start(bf16[16,32,256]{2,1,0:T(8,128)(2,1)} %bitcast.26), calls=%async_computation.5 | async-start | bytes 524288 | tf_op jit(solution)/shard_map/all_to_all | solution.py:28
  114.4 133.3 %all-gather.6.cloned.1.call-start = ((), (), s32[]{:S(2)}) async-start(), calls=%async_computation.17 | async-start | bytes 4718592 | tf_op jit(solution)/shard_map/all_gather | solution.py:308
  138.5 10.8 %all-to-all-start.7 = ((bf16[16,32,256]{2,1,0:T(8,128)(2,1)}), bf16[16,32,256]{2,1,0:T(8,128)(2,1)S(1)}, u32[]{:S(2)}, u32[]{:S(2)}) async-start(bf16[16,32,256]{2,1,0:T(8,128)(2,1)} %bitcast.116), calls=%async_computation.7 | async-start | bytes 524288 | tf_op jit(solution)/shard_map/all_to_all | solution.py:28
  149.5 15.8 %collective-permute-start.1 = (bf16[32,256]{1,0:T(8,128)(2,1)S(1)}, bf16[32,256]{1,0:T(8,128)(2,1)S(1)}, u32[]{:S(2)}, u32[]{:S(2)}) collective-permute-start(bf16[32,256]{1,0:T(8,128)(2,1)S(1)} %fusion.10), channel_id=1, source_target_pairs={{0,256},{256,0},{1,257},{257,1},{2,258},{258,2},{3,259},{259,3},{4... | collective-permute-start | bytes 49160 | tf_op jit(solution)/shard_map/ppermute | solution.py:24
  189.2 11.0 %all-to-all-start.10 = ((bf16[16,32,256]{2,1,0:T(8,128)(2,1)}), bf16[16,32,256]{2,1,0:T(8,128)(2,1)S(1)}, u32[]{:S(2)}, u32[]{:S(2)}) async-start(bf16[16,32,256]{2,1,0:T(8,128)(2,1)} %broadcast_in_dim.142), calls=%async_computation.10 | async-start | bytes 524288 | tf_op jit(solution)/shard_map/all_to_all | solution.py:28
  227.3 2.2 copy-start.3
  229.5 12.5 %copy-start.4 = (bf16[2048,1024]{1,0:T(8,128)(2,1)S(1)}, bf16[2048,1024]{1,0:T(8,128)(2,1)}, u32[]{:S(2)}) copy-start(bf16[2048,1024]{1,0:T(8,128)(2,1)} %all-gather.10.cloned.1.call-done) | copy-start | bytes 12582916
  244.1 10.9 %all-to-all-start.14 = ((bf16[16,32,256]{2,1,0:T(8,128)(2,1)}), bf16[16,32,256]{2,1,0:T(8,128)(2,1)S(1)}, u32[]{:S(2)}, u32[]{:S(2)}) async-start(bf16[16,32,256]{2,1,0:T(8,128)(2,1)} %get-tuple-element.21), calls=%async_computation.14 | async-start | bytes 524288 | tf_op jit(solution)/shard_map/all_to_all | solution.py:28
  255.0 2.2 copy-start.1
  259.3 10.8 %all-to-all-start.15 = ((bf16[16,32,256]{2,1,0:T(8,128)(2,1)}), bf16[16,32,256]{2,1,0:T(8,128)(2,1)S(1)}, u32[]{:S(2)}, u32[]{:S(2)}) async-start(bf16[16,32,256]{2,1,0:T(8,128)(2,1)} %shard_map.152), calls=%async_computation.15 | async-start | bytes 524288 | tf_op jit(solution)/shard_map/all_to_all | solution.py:28
  270.1 2.2 copy-start.2
  272.3 16.2 %copy-start.9 = (bf16[1024,256]{1,0:T(8,128)(2,1)S(1)}, bf16[1024,256]{1,0:T(8,128)(2,1)}, u32[]{:S(2)}) copy-start(bf16[1024,256]{1,0:T(8,128)(2,1)} %copy-done.8) | copy-start | bytes 1572868
Sparse Core Ops, SparseCore 0:
  10.7 76.3 all-gather.7
  95.4 63.1 all-gather.9
  160.7 62.2 all-gather.5

commit v3 on v2

--- a/solution.py
+++ b/solution.py
@@ -15,7 +15,7 @@
 WIDTH = MEMBERS * SLICE
 SMALL = (ROWS, WIDTH)
 SENT = (WAYS, ROWS, WIDTH)
-FRONT_AT, MID_AT, CORE_AT = 3, 4, 5
+FRONT_AT, MID_AT, CORE_AT, LOW_AT = 3, 4, 5, 6
 F32 = jnp.float32
 BF16 = jnp.bfloat16
 
@@ -31,10 +31,6 @@
 def gather(block, axes):
     ways = lax.axis_size(axes)
     return exchange(jnp.broadcast_to(block[None], (ways,) + block.shape), axes)
-
-
-def after(array, chain):
-    return array + jnp.minimum(jnp.abs(chain[:1, :1]), 0.0).astype(array.dtype)
 
 
 def in_order(position, own, other, axis):
@@ -113,14 +109,23 @@
     return pl.BlockSpec((MEMBERS, WIDTH, 2 * WIDTH), lambda i: (0, 0, part))
 
 
-def backward_solve(table, level, recv, weights, piece):
-    def body(table_ref, recv_ref, weights_ref, solved_ref, send_ref):
+READY = (8, 128)
+
+
+def backward_solve(table, level, recv, weights, piece, ready):
+    def body(table_ref, recv_ref, weights_ref, ready_ref, solved_ref, send_ref):
         value = apply_transposed(weights_ref, recv_ref, piece, piece)
         solved = jnp.where(packed_mask(table_ref, level, piece), value, 0.0).astype(BF16)
         solved_ref[...] = solved
         send_ref[...] = jnp.broadcast_to(solved[None], SENT)
 
-    return call(body, table, (recv, weights), [whole(SENT), weight_spec(0)], [SMALL, SENT])
+    return call(
+        body,
+        table,
+        (recv, weights, ready),
+        [whole(SENT), weight_spec(0), whole(READY)],
+        [SMALL, SENT],
+    )
 
 
 def backward_residual(table, level, recv, forward, weights, row_piece, piece):
@@ -139,8 +144,21 @@
     )[0]
 
 
-def order_shares(table, shares, chain):
-    def body(table_ref, shares_ref, chain_ref, middle_ref, matrix_ref, update_ref, root_ref):
+def order_shares(table, shares, low_matrix, low_update, chain):
+    def body(
+        table_ref,
+        shares_ref,
+        low_matrix_ref,
+        low_update_ref,
+        chain_ref,
+        middle_ref,
+        matrix_ref,
+        update_ref,
+        root_ref,
+        low_ref,
+    ):
+        low_ref[:, : 2 * WIDTH] = low_matrix_ref[...]
+        low_ref[:, 2 * WIDTH :] = low_update_ref[...]
         core = table_ref[CORE_AT]
         for o in range(2):
             block = shares_ref[table_ref[MID_AT] * 4 + o * 2 + core, :, :WIDTH]
@@ -158,24 +176,83 @@
     return call(
         body,
         table,
-        (shares, chain),
-        [whole(shares.shape), pl.BlockSpec(memory_space=pl.ANY)],
-        [(WIDTH, 4 * WIDTH), pair, pair, pair],
-    )
+        (shares, low_matrix, low_update, chain),
+        [whole(shares.shape), whole(pair), whole(pair), pl.BlockSpec(memory_space=pl.ANY)],
+        [(WIDTH, 4 * WIDTH), pair, pair, pair, (WIDTH, 4 * WIDTH)],
+    )
+
+
+def cut_rows(rows, group):
+    turned = [rows] + [pltpu.roll(rows, SLICE * d, 1) for d in range(1, MEMBERS)]
+    pieces = []
+    for target in range(MEMBERS):
+        piece = jnp.zeros((8, WIDTH), F32)
+        for q in range(8):
+            piece = jnp.where(group == q, turned[(q - target) % MEMBERS][q * 8 : q * 8 + 8], piece)
+        pieces.append(piece)
+    return pieces
+
+
+def join_rows(pieces, group, count):
+    joined = []
+    for q in range(count):
+        rows = jnp.zeros((8, WIDTH), F32)
+        for m in range(MEMBERS):
+            shift = (m - q) % MEMBERS
+            moved = pltpu.roll(pieces[m], SLICE * shift, 1) if shift else pieces[m]
+            rows = jnp.where(group == m, moved, rows)
+        joined.append(rows)
+    return joined
+
+
+def final_solve(table, level, recv, weights, piece, solved_mid, solved_top):
+    def body(table_ref, recv_ref, weights_ref, mid_ref, top_ref, send_ref):
+        value = apply_transposed(weights_ref, recv_ref, piece, piece)
+        solved = jnp.where(packed_mask(table_ref, level, piece), value, 0.0)
+        mid_rows = mid_ref[...].astype(F32)
+        mid_rows = jnp.where(table_ref[LOW_AT] == 0, mid_rows[:16], mid_rows[16:])
+        top_rows = top_ref[...].astype(F32)
+        own = table_ref[MID_AT] * 2 + table_ref[LOW_AT]
+        own_top = top_rows[:8]
+        for o in range(1, 4):
+            own_top = jnp.where(own == o, top_rows[o * 8 : o * 8 + 8], own_top)
+        rows = jnp.concatenate([solved, mid_rows, own_top, jnp.zeros((8, WIDTH), F32)], axis=0)
+        for target, cut in enumerate(cut_rows(rows, lane_group(8))):
+            send_ref[target] = cut.astype(BF16)
+
+    return call(
+        body,
+        table,
+        (recv, weights, solved_mid, solved_top),
+        [whole(SENT), weight_spec(0), whole(SMALL), whole(SMALL)],
+        [(MEMBERS, 8, WIDTH)],
+    )[0]
+
+
+def final_rows(table, recv):
+    def body(table_ref, recv_ref, low_ref, mid_ref, top_ref):
+        pieces = [recv_ref[m].astype(F32) for m in range(MEMBERS)]
+        rows = join_rows(pieces, lane_group(8), 7)
+        low_ref[...] = jnp.concatenate(rows[:4], axis=0).astype(BF16)
+        mid_ref[...] = jnp.concatenate(rows[4:6], axis=0).astype(BF16)
+        top_ref[...] = rows[6].astype(BF16)
+
+    shapes = [SMALL, (16, WIDTH), (8, WIDTH)]
+    return call(body, table, (recv,), [whole((MEMBERS, 8, WIDTH))], shapes)
 
 
 SPLIT = (MEMBERS, ROWS + 8, WIDTH)
 
 
-def root_transposed(table, recv, matrix, kept, piece):
-    def body(table_ref, recv_ref, matrix_ref, kept_ref, send_ref):
+def root_transposed(table, recv, matrix, kept, piece, ready):
+    def body(table_ref, recv_ref, matrix_ref, kept_ref, ready_ref, send_ref):
         product = jnp.dot(
             matrix_ref[...], source_rows(recv_ref, piece), preferred_element_type=F32
         )
         kept_rows = kept_ref[...].astype(F32)
         turned = [product] + [pltpu.roll(product, SLICE * d, 1) for d in range(1, MEMBERS)]
-        kept_turned = [kept_rows] + [pltpu.roll(kept_rows, SLICE * d, 1) for d in range(1, MEMBERS)]
         group = lane_group(8)
+        cut = cut_rows(kept_rows, group)
         for target in range(MEMBERS):
             blocks = []
             for o in range(ROWS // piece):
@@ -185,18 +262,14 @@
                     moved = turned[(m - target) % MEMBERS][start : start + piece]
                     rows = jnp.where(group == m, moved, rows)
                 blocks.append(rows)
-            rows = jnp.zeros((8, WIDTH), F32)
-            for q in range(8):
-                moved = kept_turned[(q - target) % MEMBERS][q * 8 : q * 8 + 8]
-                rows = jnp.where(group == q, moved, rows)
-            blocks.append(rows)
+            blocks.append(cut[target])
             send_ref[target] = jnp.concatenate(blocks, axis=0).astype(BF16)
 
     return call(
         body,
         table,
-        (recv, matrix, kept),
-        [whole(SENT), whole((WIDTH, 2 * WIDTH)), whole((2 * ROWS, WIDTH))],
+        (recv, matrix, kept, ready),
+        [whole(SENT), whole((WIDTH, 2 * WIDTH)), whole((2 * ROWS, WIDTH)), whole(READY)],
         [SPLIT],
     )[0]
 
@@ -210,27 +283,12 @@
         solved = jnp.where(packed_mask(table_ref, level, piece), total, 0.0).astype(BF16)
         solved_ref[...] = solved
         send_ref[...] = jnp.broadcast_to(solved[None], SENT)
-        group = lane_group(8)
-        kept = []
-        for q in range(8):
-            rows = jnp.zeros((8, WIDTH), F32)
-            for m in range(MEMBERS):
-                moved = blocks[m][ROWS:]
-                shift = (m - q) % MEMBERS
-                if shift:
-                    moved = pltpu.roll(moved, SLICE * shift, 1)
-                rows = jnp.where(group == m, moved, rows)
-            kept.append(rows)
+        pieces = [block[ROWS:] for block in blocks]
+        kept = join_rows(pieces, lane_group(8), 8)
         mid_ref[...] = jnp.concatenate(kept[:4], axis=0).astype(BF16)
         low_ref[...] = jnp.concatenate(kept[4:], axis=0).astype(BF16)
 
     return call(body, table, (recv,), [whole(SPLIT)], [SMALL, SMALL, SMALL, SENT])
-
-
-def from_slices(rows):
-    count = rows.shape[0]
-    sent = rows.reshape(count, MEMBERS, SLICE).transpose(1, 0, 2)
-    return exchange(sent, BLOCK).transpose(1, 0, 2).reshape(count, WIDTH)
 
 
 def shards(
@@ -267,7 +325,7 @@
 
     live_top, live_mid, live_low = live(0), live(1 + mid_pos), live(3 + mid_pos * 2 + low_pos)
     table = jnp.stack(
-        [live_top, live_mid, live_low, front_pos, mid_pos, lax.axis_index("core")]
+        [live_top, live_mid, live_low, front_pos, mid_pos, lax.axis_index("core"), low_pos]
     ).astype(jnp.int32)
     mask_top = row_mask(live_top, piece_top)
     mask_mid = row_mask(live_mid, piece_mid)
@@ -300,11 +358,12 @@
     rhs_pair = in_order(low_pos, rhs_top, shared[ROWS:], 0)
 
     columns = gather(right_mid, BLOCK)
-    middle, mid_matrix, mid_update, top_matrix = order_shares(table, shares, right_mid)
+    middle, mid_matrix, mid_update, top_matrix, low = order_shares(
+        table, shares, low_matrix, low_update, right_mid
+    )
     middle = lax.all_gather(middle, BLOCK, axis=0, tiled=False)
     forward_mid = rounded(mask_mid, product_rows(columns, mid_matrix, piece_mid, piece_mid))
 
-    low = after(jnp.concatenate([low_matrix, low_update], axis=1), forward_mid)
     low = lax.all_gather(low, BLOCK, axis=0, tiled=False)
 
     lifted = product_rows(gather(forward_mid, BLOCK), mid_update, piece_mid, piece_top)
@@ -315,27 +374,25 @@
     columns = gather(right_top, BLOCK)
     forward_top = rounded(mask_top, product_rows(columns, top_matrix, piece_top, piece_top))
     kept = jnp.concatenate([forward_mid, forward_low], axis=0)
-    sent = root_transposed(table, gather(forward_top, FRONT), top_matrix, kept, piece_top)
+    sent = root_transposed(
+        table, gather(forward_top, FRONT), top_matrix, kept, piece_top, middle[0, :8, :128]
+    )
     solution_top, forward_mid, forward_low, sent = root_collect(
         table, 0, exchange(sent, BLOCK), piece_top
     )
     sent = backward_residual(
         table, 1, exchange(sent, FRONT), forward_mid, middle, piece_top, piece_mid
     )
-    solution_mid, sent = backward_solve(table, 1, exchange(sent, FRONT), middle, piece_mid)
+    solution_mid, sent = backward_solve(
+        table, 1, exchange(sent, FRONT), middle, piece_mid, low[0, :8, :128]
+    )
     sent = backward_residual(
         table, 2, exchange(sent, FRONT), forward_low, low, piece_mid, piece_low
     )
-    solution_low, _ = backward_solve(table, 2, exchange(sent, FRONT), low, piece_low)
-
-    own_mid = lax.dynamic_slice_in_dim(solution_mid, low_pos * piece_mid, piece_mid, 0)
-    own_top = lax.dynamic_slice_in_dim(
-        solution_top, (mid_pos * 2 + low_pos) * piece_top, piece_top, 0
-    )
-    solved = from_slices(jnp.concatenate([solution_low, own_mid, own_top], axis=0))
-    solution_low = solved[:piece_low]
-    solution_mid = solved[piece_low : piece_low + piece_mid]
-    solution_top = solved[piece_low + piece_mid :]
+    sent = final_solve(
+        table, 2, exchange(sent, FRONT), low, piece_low, solution_mid, solution_top
+    )
+    solution_low, solution_mid, solution_top = final_rows(table, exchange(sent, BLOCK))
 
     moved = lax.dot_general(
         coupling, solution_low, (((0,), (0,)), ((), ())), preferred_element_type=F32

time: 301 us -> 294 us (0.977)
  blocking collectives: 127 us -> 148 us
  waiting for transfers between devices: 66.1 us -> 52.1 us
  starting transfers between devices: 47.3 us -> 41.4 us
  local copies, waits for them, and re-layouts: 20.9 us -> 15.1 us
    all_to_all x10 -> x12, blocking collectives: 127 us -> 148 us  [exchange(): return lax.all_to_all(blocks, axes, 0, 0, tiled=True)]
    all_to_all x7 -> x5, waiting for transfers between devices: 65.2 us -> 50.5 us  [exchange(): return lax.all_to_all(blocks, axes, 0, 0, tiled=True)]
    all_to_all x7 -> x5, starting transfers between devices: 26.8 us -> 19.9 us  [exchange(): return lax.all_to_all(blocks, axes, 0, 0, tiled=True)]
    unnamed x36 -> x29, local copies, waits for them, and re-layouts: 12.8 us -> 8.27 us
    pallas_call x7 -> x8, Pallas kernels: 10.7 us -> 10.9 us  [call(): pl.pallas_call(body, grid=(1,), in_specs=[pl.BlockSpec(memory_space=pltpu...]
  transfers between devices with their start and end apart: 12 -> 10, of which waited for: 8 -> 6; matrix products, arithmetic and copies ran while one was open for 6% -> 5% of each run, Pallas kernels for 2% -> 1%
where the time goes in v3:
time: 294 us; the launch traced here: 292 us
  blocking collectives  148 us (50%)
  waiting for transfers between devices  52.1 us (18%)
  starting transfers between devices  41.4 us (14%)
  local copies, waits for them, and re-layouts  15.1 us (5%)
  between operations  14.1 us (5%)
  Pallas kernels  10.9 us (4%)
  other arithmetic  5.69 us (2%)
  matrix products  5.13 us (2%)
    all_to_all x12, blocking collectives, exchange(): return lax.all_to_all(blocks, axes, 0, 0, tiled=True)  148 us
    all_to_all x5, waiting for transfers between devices, exchange(): return lax.all_to_all(blocks, axes, 0, 0, tiled=True)  50.5 us
    ppermute x2, starting transfers between devices, swap(): return lax.ppermute(array, axis, [(0, 1), (1, 0)])  21.4 us
    all_to_all x5, starting transfers between devices, exchange(): return lax.all_to_all(blocks, axes, 0, 0, tiled=True)  19.9 us
    pallas_call x8, Pallas kernels, call(): pl.pallas_call(body, grid=(1,), in_specs=[pl.BlockSpec(memory_space=pltpu...  10.9 us
    unnamed x29, local copies, waits for them, and re-layouts  8.27 us
  transfers between devices with their start and end apart: 10, of which 6 were waited for; matrix products, arithmetic and copies ran while one was open for 5% of the time, Pallas kernels for 1%

profile of v3, /device:TPU:1, one launch (start us, length us, event | category | flops | bytes accessed | tf_op | source)
XLA Modules:
  0.0 292.3 jit_solution(3000844198461421871)
XLA Ops:
  7.2 1.1 copy.43
  8.3 1.7 pad_maximum_fusion
  10.0 1.4 fusion.23
  11.4 0.7 fusion.17
  12.1 1.8 convolution_convert_fusion.1
  13.9 0.2 fusion.7
  14.2 15.2 %all_to_all.85 = bf16[8,32,256]{2,1,0:T(8,128)(2,1)S(1)} all-to-all(bf16[8,32,256]{2,1,0:T(8,128)(2,1)S(1)} %broadcast_in_dim.132), channel_id=1, replica_groups=mesh['mid'=2,'low'=2,'z'=4,'core'=2,'x'=4,'y'=4] {'z','core'}, dimensions={0} | all-to-all | bytes 262144 | tf_op jit(solution)/shard_map/all_to_all | solution.py:28
  29.4 0.2 fusion.3
  29.6 0.1 copy.24
  29.8 12.0 %all_to_all.86 = bf16[16,32,256]{2,1,0:T(8,128)(2,1)S(1)} all-to-all(bf16[16,32,256]{2,1,0:T(8,128)(2,1)S(1)} %bitcast.124), channel_id=1, replica_groups=mesh['mid'=2,'low'=2,'z'=4,'core'=2,'x'=4,'y'=4] {'x','y'}, dimensions={0} | all-to-all | bytes 524288 | tf_op jit(solution)/shard_map/all_to_all | solution.py:28
  41.9 0.1 select_convert_fusion.4
  41.9 0.7 broadcast_in_dim.133
  42.6 5.5 %all-to-all-start.2 = ((bf16[8,32,256]{2,1,0:T(8,128)(2,1)}), bf16[8,32,256]{2,1,0:T(8,128)(2,1)S(1)}, u32[]{:S(2)}, u32[]{:S(2)}) async-start(bf16[8,32,256]{2,1,0:T(8,128)(2,1)} %broadcast_in_dim.133), calls=%async_computation.2 | async-start | bytes 262144 | tf_op jit(solution)/shard_map/all_to_all | solution.py:28
  48.1 22.6 %all-to-all-done.2 = bf16[8,32,256]{2,1,0:T(8,128)(2,1)S(1)} async-done(((bf16[8,32,256]{2,1,0:T(8,128)(2,1)}), bf16[8,32,256]{2,1,0:T(8,128)(2,1)S(1)}, u32[]{:S(2)}, u32[]{:S(2)}) %all-to-all-start.2) | async-done | bytes 131104 | tf_op jit(solution)/shard_map/all_to_all | solution.py:28
  70.8 0.2 fusion.4
  71.0 0.1 copy.25
  71.2 0.7 copy.26
  71.9 3.5 %all-to-all-start.3 = ((bf16[16,32,256]{2,1,0:T(8,128)(2,1)}), bf16[16,32,256]{2,1,0:T(8,128)(2,1)S(1)}, u32[]{:S(2)}, u32[]{:S(2)}) async-start(bf16[16,32,256]{2,1,0:T(8,128)(2,1)} %bitcast.20), calls=%async_computation.3 | async-start | bytes 524288 | tf_op jit(solution)/shard_map/all_to_all | solution.py:28
  75.6 0.1 broadcast_in_dim.126
  75.7 7.3 %all-to-all-done.3 = bf16[16,32,256]{2,1,0:T(8,128)(2,1)S(1)} async-done(((bf16[16,32,256]{2,1,0:T(8,128)(2,1)}), bf16[16,32,256]{2,1,0:T(8,128)(2,1)S(1)}, u32[]{:S(2)}, u32[]{:S(2)}) %all-to-all-start.3) | async-done | bytes 262176 | tf_op jit(solution)/shard_map/all_to_all | solution.py:28
  83.1 6.1 %collective-permute-start = (bf16[40,256]{1,0:T(8,128)(2,1)S(1)}, bf16[40,256]{1,0:T(8,128)(2,1)S(1)}, u32[]{:S(2)}, u32[]{:S(2)}) collective-permute-start(bf16[40,256]{1,0:T(8,128)(2,1)S(1)} %pad_maximum_fusion.2), channel_id=1, source_target_pairs={{0,128},{128,0},{1,129},{129,1},{2,130},{130,2},{3,131},{131,3},{4... | collective-permute-start | bytes 61448 | tf_op jit(solution)/shard_map/ppermute | solution.py:24
  89.1 0.6 fusion.18
  89.8 1.9 stack.31.table_ref
  91.7 1.7 copy-done.4
  93.5 1.8 shard_map.147
  95.3 0.7 all-gather.11.cloned.1.call-update
  96.0 14.4 %all_to_all.87 = bf16[8,32,256]{2,1,0:T(8,128)(2,1)S(1)} all-to-all(bf16[8,32,256]{2,1,0:T(8,128)(2,1)S(1)} %broadcast_in_dim.139), channel_id=1, replica_groups=mesh['mid'=2,'low'=2,'z'=4,'core'=2,'x'=4,'y'=4] {'z','core'}, dimensions={0} | all-to-all | bytes 262144 | tf_op jit(solution)/shard_map/all_to_all | solution.py:28
  110.4 0.3 convolution_convert_fusion.4
  110.7 10.6 %all_to_all.88 = bf16[16,32,256]{2,1,0:T(8,128)(2,1)S(1)} all-to-all(bf16[16,32,256]{2,1,0:T(8,128)(2,1)S(1)} %bitcast.126), channel_id=1, replica_groups=mesh['mid'=2,'low'=2,'z'=4,'core'=2,'x'=4,'y'=4] {'x','y'}, dimensions={0} | all-to-all | bytes 524288 | tf_op jit(solution)/shard_map/all_to_all | solution.py:28
  121.5 12.6 %all_to_all.89 = bf16[8,32,256]{2,1,0:T(8,128)(2,1)S(1)} all-to-all(bf16[8,32,256]{2,1,0:T(8,128)(2,1)S(1)} %broadcast_in_dim.140), channel_id=1, replica_groups=mesh['mid'=2,'low'=2,'z'=4,'core'=2,'x'=4,'y'=4] {'z','core'}, dimensions={0} | all-to-all | bytes 262144 | tf_op jit(solution)/shard_map/all_to_all | solution.py:28
  134.1 0.3 convolution_convert_fusion.3
  134.3 0.7 copy.42
  135.1 3.5 %all-to-all-start.7 = ((bf16[16,32,256]{2,1,0:T(8,128)(2,1)}), bf16[16,32,256]{2,1,0:T(8,128)(2,1)S(1)}, u32[]{:S(2)}, u32[]{:S(2)}) async-start(bf16[16,32,256]{2,1,0:T(8,128)(2,1)} %bitcast.109), calls=%async_computation.7 | async-start | bytes 524288 | tf_op jit(solution)/shard_map/all_to_all | solution.py:28
  138.7 0.1 broadcast_in_dim.135
  138.8 7.1 %all-to-all-done.7 = bf16[16,32,256]{2,1,0:T(8,128)(2,1)S(1)} async-done(((bf16[16,32,256]{2,1,0:T(8,128)(2,1)}), bf16[16,32,256]{2,1,0:T(8,128)(2,1)S(1)}, u32[]{:S(2)}, u32[]{:S(2)}) %all-to-all-start.7) | async-done | bytes 262176 | tf_op jit(solution)/shard_map/all_to_all | solution.py:28
  146.0 15.4 %collective-permute-start.1 = (bf16[32,256]{1,0:T(8,128)(2,1)S(1)}, bf16[32,256]{1,0:T(8,128)(2,1)S(1)}, u32[]{:S(2)}, u32[]{:S(2)}) collective-permute-start(bf16[32,256]{1,0:T(8,128)(2,1)S(1)} %fusion.10), channel_id=1, source_target_pairs={{0,256},{256,0},{1,257},{257,1},{2,258},{258,2},{3,259},{259,3},{4... | collective-permute-start | bytes 49160 | tf_op jit(solution)/shard_map/ppermute | solution.py:24
  161.4 0.6 fusion.19
  162.0 0.9 collective-permute-done.1
  162.9 11.9 %all_to_all.90 = bf16[8,32,256]{2,1,0:T(8,128)(2,1)S(1)} all-to-all(bf16[8,32,256]{2,1,0:T(8,128)(2,1)S(1)} %broadcast_in_dim.141), channel_id=1, replica_groups=mesh['mid'=2,'low'=2,'z'=4,'core'=2,'x'=4,'y'=4] {'z','core'}, dimensions={0} | all-to-all | bytes 262144 | tf_op jit(solution)/shard_map/all_to_all | solution.py:28
  174.8 0.3 convolution_convert_fusion.2
  175.1 10.6 %all_to_all.91 = bf16[16,32,256]{2,1,0:T(8,128)(2,1)S(1)} all-to-all(bf16[16,32,256]{2,1,0:T(8,128)(2,1)S(1)} %bitcast.128), channel_id=1, replica_groups=mesh['mid'=2,'low'=2,'z'=4,'core'=2,'x'=4,'y'=4] {'x','y'}, dimensions={0} | all-to-all | bytes 524288 | tf_op jit(solution)/shard_map/all_to_all | solution.py:28
  185.9 0.7 broadcast_in_dim.142
  186.6 3.5 %all-to-all-start.10 = ((bf16[16,32,256]{2,1,0:T(8,128)(2,1)}), bf16[16,32,256]{2,1,0:T(8,128)(2,1)S(1)}, u32[]{:S(2)}, u32[]{:S(2)}) async-start(bf16[16,32,256]{2,1,0:T(8,128)(2,1)} %broadcast_in_dim.142), calls=%async_computation.10 | async-start | bytes 524288 | tf_op jit(solution)/shard_map/all_to_all | solution.py:28
  190.2 0.7 slice_bitcast_fusion.1.ready_ref
  190.9 6.7 %all-to-all-done.10.recv_ref = bf16[16,32,256]{2,1,0:T(8,128)(2,1)S(1)} async-done(((bf16[16,32,256]{2,1,0:T(8,128)(2,1)}), bf16[16,32,256]{2,1,0:T(8,128)(2,1)S(1)}, u32[]{:S(2)}, u32[]{:S(2)}) %all-to-all-start.10) | async-done | bytes 262176 | tf_op jit(solution)/shard_map/all_to_all | solution.py:28
  197.6 0.9 shard_map.148
  198.5 15.1 %all_to_all.92.recv_ref = bf16[8,40,256]{2,1,0:T(8,128)(2,1)S(1)} all-to-all(bf16[8,40,256]{2,1,0:T(8,128)(2,1)S(1)} %shard_map.148), channel_id=1, replica_groups=mesh['mid'=2,'low'=2,'z'=4,'core'=2,'x'=4,'y'=4] {'z','core'}, dimensions={0} | all-to-all | bytes 327680 | tf_op jit(solution)/shard_map/all_to_all | solution.py:28
  213.6 0.6 shard_map.149
  214.3 10.5 %all_to_all.93.recv_ref = bf16[16,32,256]{2,1,0:T(8,128)(2,1)S(1)} all-to-all(bf16[16,32,256]{2,1,0:T(8,128)(2,1)S(1)} %get-tuple-element.22), channel_id=1, replica_groups=mesh['mid'=2,'low'=2,'z'=4,'core'=2,'x'=4,'y'=4] {'x','y'}, dimensions={0} | all-to-all | bytes 524288 | tf_op jit(solution)/shard_map/all_to_all | solution.py:28
  224.8 2.2 copy-done.2
  227.0 2.1 shard_map.150
  229.1 3.8 %all-to-all-start.13 = ((bf16[16,32,256]{2,1,0:T(8,128)(2,1)}), bf16[16,32,256]{2,1,0:T(8,128)(2,1)S(1)}, u32[]{:S(2)}, u32[]{:S(2)}) async-start(bf16[16,32,256]{2,1,0:T(8,128)(2,1)} %shard_map.150), calls=%async_computation.13 | async-start | bytes 524288 | tf_op jit(solution)/shard_map/all_to_all | solution.py:28
  232.9 0.7 slice_bitcast_fusion.ready_ref
  233.6 6.8 %all-to-all-done.13.recv_ref = bf16[16,32,256]{2,1,0:T(8,128)(2,1)S(1)} async-done(((bf16[16,32,256]{2,1,0:T(8,128)(2,1)}), bf16[16,32,256]{2,1,0:T(8,128)(2,1)S(1)}, u32[]{:S(2)}, u32[]{:S(2)}) %all-to-all-start.13) | async-done | bytes 262176 | tf_op jit(solution)/shard_map/all_to_all | solution.py:28
  240.4 2.2 copy-done.3
  242.6 1.4 shard_map.151
  244.0 10.7 %all_to_all.94.recv_ref = bf16[16,32,256]{2,1,0:T(8,128)(2,1)S(1)} all-to-all(bf16[16,32,256]{2,1,0:T(8,128)(2,1)S(1)} %get-tuple-element.25), channel_id=1, replica_groups=mesh['mid'=2,'low'=2,'z'=4,'core'=2,'x'=4,'y'=4] {'x','y'}, dimensions={0} | all-to-all | bytes 524288 | tf_op jit(solution)/shard_map/all_to_all | solution.py:28
  254.6 1.4 shard_map.152
  256.0 10.5 %all_to_all.95.recv_ref = bf16[16,32,256]{2,1,0:T(8,128)(2,1)S(1)} all-to-all(bf16[16,32,256]{2,1,0:T(8,128)(2,1)S(1)} %shard_map.152), channel_id=1, replica_groups=mesh['mid'=2,'low'=2,'z'=4,'core'=2,'x'=4,'y'=4] {'x','y'}, dimensions={0} | all-to-all | bytes 524288 | tf_op jit(solution)/shard_map/all_to_all | solution.py:28
  266.5 1.5 shard_map.153
  268.0 13.6 %all_to_all.96.recv_ref = bf16[8,8,256]{2,1,0:T(8,128)(2,1)S(1)} all-to-all(bf16[8,8,256]{2,1,0:T(8,128)(2,1)S(1)} %shard_map.153), channel_id=1, replica_groups=mesh['mid'=2,'low'=2,'z'=4,'core'=2,'x'=4,'y'=4] {'z','core'}, dimensions={0} | all-to-all | bytes 65536 | tf_op jit(solution)/shard_map/all_to_all | solution.py:28
  281.6 1.2 shard_map.154
  282.9 1.9 fusion.2
  284.7 1.0 copy.34
  (62 shorter events, 1.2 us)
Async XLA Ops:
  7.2 4.9 %copy-start = (bf16[1024,1024]{1,0:T(8,128)(2,1)S(1)}, bf16[1024,1024]{1,0:T(8,128)(2,1)}, u32[]{:S(2)}) copy-start(bf16[1024,1024]{1,0:T(8,128)(2,1)} %param.13) | copy-start | bytes 6291460
  7.2 84.6 %all-gather.7.cloned.1.call-start = ((), (), s32[]{:S(2)}) async-start(), calls=%async_computation.17 | async-start | bytes 2949120 | tf_op jit(solution)/shard_map/all_gather | solution.py:349
  12.1 1.8 copy-start.9
  12.1 1.8 copy-start.10
  12.1 17.3 %copy-start.5 = (bf16[8,1,32,512]{3,2,1,0:T(8,128)(2,1)S(1)}, bf16[8,1,32,512]{3,2,1,0:T(8,128)(2,1)}, u32[]{:S(2)}) copy-start(bf16[8,1,32,512]{3,2,1,0:T(8,128)(2,1)} %param.20) | copy-start | bytes 786436
  13.9 15.5 %copy-start.6 = (bf16[1024,256]{1,0:T(8,128)(2,1)}, bf16[1024,256]{1,0:T(8,128)(2,1)S(1)}, u32[]{:S(2)}) copy-start(bf16[1024,256]{1,0:T(8,128)(2,1)S(1)} %convolution_convert_fusion.1) | copy-start | bytes 1572868
  13.9 34.2 %copy-start.8 = (bf16[8,1,32,2,256]{4,3,2,1,0:T(2,128)(2,1)S(1)}, bf16[8,1,32,2,256]{4,3,2,1,0:T(2,128)(2,1)}, u32[]{:S(2)}) copy-start(bf16[8,1,32,2,256]{4,3,2,1,0:T(2,128)(2,1)} %param.22) | copy-start | bytes 786436
  29.8 45.9 %copy-start.12 = (bf16[16,256]{1,0:T(8,128)(2,1)S(1)}, bf16[16,256]{1,0:T(8,128)(2,1)}, u32[]{:S(2)}) copy-start(bf16[16,256]{1,0:T(8,128)(2,1)} %param.16) | copy-start | bytes 24580
  29.8 53.3 %copy-start.11 = (bf16[8,256]{1,0:T(8,128)(2,1)S(1)}, bf16[8,256]{1,0:T(8,128)(2,1)}, u32[]{:S(2)}) copy-start(bf16[8,256]{1,0:T(8,128)(2,1)} %param.15) | copy-start | bytes 12292
  42.6 28.2 %all-to-all-start.2 = ((bf16[8,32,256]{2,1,0:T(8,128)(2,1)}), bf16[8,32,256]{2,1,0:T(8,128)(2,1)S(1)}, u32[]{:S(2)}, u32[]{:S(2)}) async-start(bf16[8,32,256]{2,1,0:T(8,128)(2,1)} %broadcast_in_dim.133), calls=%async_computation.2 | async-start | bytes 262144 | tf_op jit(solution)/shard_map/all_to_all | solution.py:28
  71.9 11.0 %all-to-all-start.3 = ((bf16[16,32,256]{2,1,0:T(8,128)(2,1)}), bf16[16,32,256]{2,1,0:T(8,128)(2,1)S(1)}, u32[]{:S(2)}, u32[]{:S(2)}) async-start(bf16[16,32,256]{2,1,0:T(8,128)(2,1)} %bitcast.20), calls=%async_computation.3 | async-start | bytes 524288 | tf_op jit(solution)/shard_map/all_to_all | solution.py:28
  75.4 114.8 %all-gather.9.cloned.1.call-start = ((), (), s32[]{:S(2)}) async-start(), calls=%async_computation.18 | async-start | bytes 4718592 | tf_op jit(solution)/shard_map/all_gather | solution.py:364
  83.1 8.6 %collective-permute-start = (bf16[40,256]{1,0:T(8,128)(2,1)S(1)}, bf16[40,256]{1,0:T(8,128)(2,1)S(1)}, u32[]{:S(2)}, u32[]{:S(2)}) collective-permute-start(bf16[40,256]{1,0:T(8,128)(2,1)S(1)} %pad_maximum_fusion.2), channel_id=1, source_target_pairs={{0,128},{128,0},{1,129},{129,1},{2,130},{130,2},{3,131},{131,3},{4... | collective-permute-start | bytes 61448 | tf_op jit(solution)/shard_map/ppermute | solution.py:24
  91.7 1.7 copy-start.4
  95.3 137.6 %all-gather.11.cloned.1.call-start = ((), (), s32[]{:S(2)}) async-start(), calls=%async_computation.19 | async-start | bytes 4718592 | tf_op jit(solution)/shard_map/all_gather | solution.py:367
  135.1 10.8 %all-to-all-start.7 = ((bf16[16,32,256]{2,1,0:T(8,128)(2,1)}), bf16[16,32,256]{2,1,0:T(8,128)(2,1)S(1)}, u32[]{:S(2)}, u32[]{:S(2)}) async-start(bf16[16,32,256]{2,1,0:T(8,128)(2,1)} %bitcast.109), calls=%async_computation.7 | async-start | bytes 524288 | tf_op jit(solution)/shard_map/all_to_all | solution.py:28
  146.0 16.8 %collective-permute-start.1 = (bf16[32,256]{1,0:T(8,128)(2,1)S(1)}, bf16[32,256]{1,0:T(8,128)(2,1)S(1)}, u32[]{:S(2)}, u32[]{:S(2)}) collective-permute-start(bf16[32,256]{1,0:T(8,128)(2,1)S(1)} %fusion.10), channel_id=1, source_target_pairs={{0,256},{256,0},{1,257},{257,1},{2,258},{258,2},{3,259},{259,3},{4... | collective-permute-start | bytes 49160 | tf_op jit(solution)/shard_map/ppermute | solution.py:24
  186.6 11.0 %all-to-all-start.10 = ((bf16[16,32,256]{2,1,0:T(8,128)(2,1)}), bf16[16,32,256]{2,1,0:T(8,128)(2,1)S(1)}, u32[]{:S(2)}, u32[]{:S(2)}) async-start(bf16[16,32,256]{2,1,0:T(8,128)(2,1)} %broadcast_in_dim.142), calls=%async_computation.10 | async-start | bytes 524288 | tf_op jit(solution)/shard_map/all_to_all | solution.py:28
  224.8 2.2 copy-start.2
  229.1 11.3 %all-to-all-start.13 = ((bf16[16,32,256]{2,1,0:T(8,128)(2,1)}), bf16[16,32,256]{2,1,0:T(8,128)(2,1)S(1)}, u32[]{:S(2)}, u32[]{:S(2)}) async-start(bf16[16,32,256]{2,1,0:T(8,128)(2,1)} %shard_map.150), calls=%async_computation.13 | async-start | bytes 524288 | tf_op jit(solution)/shard_map/all_to_all | solution.py:28
  240.4 2.2 copy-start.3
  242.6 12.1 %copy-start.1 = (bf16[2048,1024]{1,0:T(8,128)(2,1)S(1)}, bf16[2048,1024]{1,0:T(8,128)(2,1)}, u32[]{:S(2)}) copy-start(bf16[2048,1024]{1,0:T(8,128)(2,1)} %all-gather.11.cloned.1.call-done) | copy-start | bytes 12582916
  266.5 16.3 %copy-start.7 = (bf16[1024,256]{1,0:T(8,128)(2,1)S(1)}, bf16[1024,256]{1,0:T(8,128)(2,1)}, u32[]{:S(2)}) copy-start(bf16[1024,256]{1,0:T(8,128)(2,1)} %copy-done.6) | copy-start | bytes 1572868
Sparse Core Ops, SparseCore 0:
  10.7 76.3 all-gather.6
  95.4 64.0 all-gather.8
  161.6 62.4 all-gather.10

commit v4 on v3

--- a/solution.py
+++ b/solution.py
@@ -128,7 +128,7 @@
     )
 
 
-def backward_residual(table, level, recv, forward, weights, row_piece, piece):
+def backward_residual(table, level, recv, forward, weights, part, row_piece, piece):
     def body(table_ref, recv_ref, forward_ref, weights_ref, send_ref):
         value = forward_ref[...].astype(F32)
         value = value - apply_transposed(weights_ref, recv_ref, row_piece, piece)
@@ -139,7 +139,7 @@
         body,
         table,
         (recv, forward, weights),
-        [whole(SENT), whole(SMALL), weight_spec(1)],
+        [whole(SENT), whole(SMALL), weight_spec(part)],
         [SENT],
     )[0]
 
@@ -151,7 +151,6 @@
         low_matrix_ref,
         low_update_ref,
         chain_ref,
-        middle_ref,
         matrix_ref,
         update_ref,
         root_ref,
@@ -163,12 +162,10 @@
         for o in range(2):
             block = shares_ref[table_ref[MID_AT] * 4 + o * 2 + core, :, :WIDTH]
             matrix_ref[:, o * WIDTH : (o + 1) * WIDTH] = block
-            middle_ref[:, o * WIDTH : (o + 1) * WIDTH] = block
             for h in range(2):
                 block = shares_ref[table_ref[MID_AT] * 4 + o * 2 + core, :, WIDTH + h * 128 : WIDTH + h * 128 + 128]
                 start = (h * 2 + o) * 128
                 update_ref[:, start : start + 128] = block
-                middle_ref[:, 2 * WIDTH + start : 2 * WIDTH + start + 128] = block
         for o in range(4):
             root_ref[:, o * 128 : o * 128 + 128] = shares_ref[o * 2 + core, :, 2 * WIDTH :]
 
@@ -178,7 +175,7 @@
         table,
         (shares, low_matrix, low_update, chain),
         [whole(shares.shape), whole(pair), whole(pair), pl.BlockSpec(memory_space=pl.ANY)],
-        [(WIDTH, 4 * WIDTH), pair, pair, pair, (WIDTH, 4 * WIDTH)],
+        [pair, pair, pair, (WIDTH, 4 * WIDTH)],
     )
 
 
@@ -358,10 +355,11 @@
     rhs_pair = in_order(low_pos, rhs_top, shared[ROWS:], 0)
 
     columns = gather(right_mid, BLOCK)
-    middle, mid_matrix, mid_update, top_matrix, low = order_shares(
+    mid_matrix, mid_update, top_matrix, low = order_shares(
         table, shares, low_matrix, low_update, right_mid
     )
-    middle = lax.all_gather(middle, BLOCK, axis=0, tiled=False)
+    all_update = lax.all_gather(mid_update, BLOCK, axis=0, tiled=False)
+    all_matrix = lax.all_gather(mid_matrix, BLOCK, axis=0, tiled=False)
     forward_mid = rounded(mask_mid, product_rows(columns, mid_matrix, piece_mid, piece_mid))
 
     low = lax.all_gather(low, BLOCK, axis=0, tiled=False)
@@ -375,19 +373,19 @@
     forward_top = rounded(mask_top, product_rows(columns, top_matrix, piece_top, piece_top))
     kept = jnp.concatenate([forward_mid, forward_low], axis=0)
     sent = root_transposed(
-        table, gather(forward_top, FRONT), top_matrix, kept, piece_top, middle[0, :8, :128]
+        table, gather(forward_top, FRONT), top_matrix, kept, piece_top, all_update[0, :8, :128]
     )
     solution_top, forward_mid, forward_low, sent = root_collect(
         table, 0, exchange(sent, BLOCK), piece_top
     )
     sent = backward_residual(
-        table, 1, exchange(sent, FRONT), forward_mid, middle, piece_top, piece_mid
+        table, 1, exchange(sent, FRONT), forward_mid, all_update, 0, piece_top, piece_mid
     )
     solution_mid, sent = backward_solve(
-        table, 1, exchange(sent, FRONT), middle, piece_mid, low[0, :8, :128]
+        table, 1, exchange(sent, FRONT), all_matrix, piece_mid, low[0, :8, :128]
     )
     sent = backward_residual(
-        table, 2, exchange(sent, FRONT), forward_low, low, piece_mid, piece_low
+        table, 2, exchange(sent, FRONT), forward_low, low, 1, piece_mid, piece_low
     )
     sent = final_solve(
         table, 2, exchange(sent, FRONT), low, piece_low, solution_mid, solution_top

time: 294 us -> 311 us (1.058)
  waiting for transfers between devices: 52.1 us -> 71.6 us
  blocking collectives: 148 us -> 137 us
  starting transfers between devices: 41.4 us -> 46.3 us
    all_gather x1 -> x2, waiting for transfers between devices: 0.02 us -> 19.3 us  [the longest x1 19.3 us: shards(): all_matrix = lax.all_gather(mid_matrix, BLOCK, axis=0, tiled=False)]
    all_to_all x12 -> x11, blocking collectives: 148 us -> 137 us  [exchange(): return lax.all_to_all(blocks, axes, 0, 0, tiled=True)]
    all_to_all x5 -> x6, starting transfers between devices: 19.9 us -> 25.5 us  [exchange(): return lax.all_to_all(blocks, axes, 0, 0, tiled=True)]
    all_to_all x5 -> x6, waiting for transfers between devices: 50.5 us -> 50.5 us  [exchange(): return lax.all_to_all(blocks, axes, 0, 0, tiled=True)]
  transfers between devices with their start and end apart: 10 -> 12, of which waited for: 6 -> 7; matrix products, arithmetic and copies ran while one was open for 5% -> 5% of each run, Pallas kernels for 1% -> 1%
where the time goes in v4:
time: 311 us; the launch traced here: 309 us
  blocking collectives  137 us (44%)
  waiting for transfers between devices  71.6 us (23%)
  starting transfers between devices  46.3 us (15%)
  local copies, waits for them, and re-layouts  16.9 us (5%)
  between operations  14.2 us (5%)
  Pallas kernels  10.8 us (3%)
  matrix products  7.05 us (2%)
  other arithmetic  5.8 us (2%)
    all_to_all x11, blocking collectives, exchange(): return lax.all_to_all(blocks, axes, 0, 0, tiled=True)  137 us
    all_to_all x6, waiting for transfers between devices, exchange(): return lax.all_to_all(blocks, axes, 0, 0, tiled=True)  50.5 us
    all_to_all x6, starting transfers between devices, exchange(): return lax.all_to_all(blocks, axes, 0, 0, tiled=True)  25.5 us
    ppermute x2, starting transfers between devices, swap(): return lax.ppermute(array, axis, [(0, 1), (1, 0)])  20.7 us
    all_gather x1, waiting for transfers between devices, shards(): all_matrix = lax.all_gather(mid_matrix, BLOCK, axis=0, tiled=False)  19.3 us
    pallas_call x8, Pallas kernels, call(): pl.pallas_call(body, grid=(1,), in_specs=[pl.BlockSpec(memory_space=pltpu...  10.8 us
    unnamed x29, local copies, waits for them, and re-layouts  9.35 us
  transfers between devices with their start and end apart: 12, of which 7 were waited for; matrix products, arithmetic and copies ran while one was open for 5% of the time, Pallas kernels for 1%

profile of v4, /device:TPU:1, one launch (start us, length us, event | category | flops | bytes accessed | tf_op | source)
XLA Modules:
  0.0 309.2 jit_solution(7586179225169571470)
XLA Ops:
  7.2 1.1 copy.43
  8.3 1.7 pad_maximum_fusion
  10.0 1.4 fusion.23
  11.4 0.7 fusion.17
  12.1 1.8 convolution_convert_fusion.1
  14.0 0.2 fusion.7
  14.2 15.2 %all_to_all.85 = bf16[8,32,256]{2,1,0:T(8,128)(2,1)S(1)} all-to-all(bf16[8,32,256]{2,1,0:T(8,128)(2,1)S(1)} %broadcast_in_dim.132), channel_id=1, replica_groups=mesh['mid'=2,'low'=2,'z'=4,'core'=2,'x'=4,'y'=4] {'z','core'}, dimensions={0} | all-to-all | bytes 262144 | tf_op jit(solution)/shard_map/all_to_all | solution.py:28
  29.4 0.2 fusion.3
  29.7 0.1 copy.24
  29.8 12.0 %all_to_all.86 = bf16[16,32,256]{2,1,0:T(8,128)(2,1)S(1)} all-to-all(bf16[16,32,256]{2,1,0:T(8,128)(2,1)S(1)} %bitcast.123), channel_id=1, replica_groups=mesh['mid'=2,'low'=2,'z'=4,'core'=2,'x'=4,'y'=4] {'x','y'}, dimensions={0} | all-to-all | bytes 524288 | tf_op jit(solution)/shard_map/all_to_all | solution.py:28
  42.0 0.7 broadcast_in_dim.133
  42.6 5.5 %all-to-all-start.2 = ((bf16[8,32,256]{2,1,0:T(8,128)(2,1)}), bf16[8,32,256]{2,1,0:T(8,128)(2,1)S(1)}, u32[]{:S(2)}, u32[]{:S(2)}) async-start(bf16[8,32,256]{2,1,0:T(8,128)(2,1)} %broadcast_in_dim.133), calls=%async_computation.2 | async-start | bytes 262144 | tf_op jit(solution)/shard_map/all_to_all | solution.py:28
  48.2 22.6 %all-to-all-done.2 = bf16[8,32,256]{2,1,0:T(8,128)(2,1)S(1)} async-done(((bf16[8,32,256]{2,1,0:T(8,128)(2,1)}), bf16[8,32,256]{2,1,0:T(8,128)(2,1)S(1)}, u32[]{:S(2)}, u32[]{:S(2)}) %all-to-all-start.2) | async-done | bytes 131104 | tf_op jit(solution)/shard_map/all_to_all | solution.py:28
  70.8 0.2 fusion.4
  71.2 0.8 copy.26
  71.9 3.5 %all-to-all-start.3 = ((bf16[16,32,256]{2,1,0:T(8,128)(2,1)}), bf16[16,32,256]{2,1,0:T(8,128)(2,1)S(1)}, u32[]{:S(2)}, u32[]{:S(2)}) async-start(bf16[16,32,256]{2,1,0:T(8,128)(2,1)} %bitcast.20), calls=%async_computation.3 | async-start | bytes 524288 | tf_op jit(solution)/shard_map/all_to_all | solution.py:28
  75.7 7.3 %all-to-all-done.3 = bf16[16,32,256]{2,1,0:T(8,128)(2,1)S(1)} async-done(((bf16[16,32,256]{2,1,0:T(8,128)(2,1)}), bf16[16,32,256]{2,1,0:T(8,128)(2,1)S(1)}, u32[]{:S(2)}, u32[]{:S(2)}) %all-to-all-start.3) | async-done | bytes 262176 | tf_op jit(solution)/shard_map/all_to_all | solution.py:28
  83.1 6.1 %collective-permute-start = (bf16[40,256]{1,0:T(8,128)(2,1)S(1)}, bf16[40,256]{1,0:T(8,128)(2,1)S(1)}, u32[]{:S(2)}, u32[]{:S(2)}) collective-permute-start(bf16[40,256]{1,0:T(8,128)(2,1)S(1)} %pad_maximum_fusion.2), channel_id=1, source_target_pairs={{0,128},{128,0},{1,129},{129,1},{2,130},{130,2},{3,131},{131,3},{4... | collective-permute-start | bytes 61448 | tf_op jit(solution)/shard_map/ppermute | solution.py:24
  89.2 0.7 fusion.18
  89.9 2.0 stack.31.table_ref
  91.9 1.7 copy-done.2
  93.7 1.6 shard_map.147
  95.3 0.7 all-gather.15.cloned.1.call-update
  96.0 14.5 %all_to_all.87 = bf16[8,32,256]{2,1,0:T(8,128)(2,1)S(1)} all-to-all(bf16[8,32,256]{2,1,0:T(8,128)(2,1)S(1)} %broadcast_in_dim.139), channel_id=1, replica_groups=mesh['mid'=2,'low'=2,'z'=4,'core'=2,'x'=4,'y'=4] {'z','core'}, dimensions={0} | all-to-all | bytes 262144 | tf_op jit(solution)/shard_map/all_to_all | solution.py:28
  110.6 1.2 convolution_convert_fusion.4
  111.8 10.6 %all_to_all.88 = bf16[16,32,256]{2,1,0:T(8,128)(2,1)S(1)} all-to-all(bf16[16,32,256]{2,1,0:T(8,128)(2,1)S(1)} %bitcast.126), channel_id=1, replica_groups=mesh['mid'=2,'low'=2,'z'=4,'core'=2,'x'=4,'y'=4] {'x','y'}, dimensions={0} | all-to-all | bytes 524288 | tf_op jit(solution)/shard_map/all_to_all | solution.py:28
  122.6 0.7 broadcast_in_dim.140
  123.2 5.6 %all-to-all-start.6 = ((bf16[8,32,256]{2,1,0:T(8,128)(2,1)}), bf16[8,32,256]{2,1,0:T(8,128)(2,1)S(1)}, u32[]{:S(2)}, u32[]{:S(2)}) async-start(bf16[8,32,256]{2,1,0:T(8,128)(2,1)} %broadcast_in_dim.140), calls=%async_computation.6 | async-start | bytes 262144 | tf_op jit(solution)/shard_map/all_to_all | solution.py:28
  128.8 0.6 all-gather.13.cloned.1.call-update
  129.4 6.9 %all-to-all-done.6 = bf16[8,32,256]{2,1,0:T(8,128)(2,1)S(1)} async-done(((bf16[8,32,256]{2,1,0:T(8,128)(2,1)}), bf16[8,32,256]{2,1,0:T(8,128)(2,1)S(1)}, u32[]{:S(2)}, u32[]{:S(2)}) %all-to-all-start.6) | async-done | bytes 131104 | tf_op jit(solution)/shard_map/all_to_all | solution.py:28
  136.3 1.2 convolution_convert_fusion.3
  137.5 0.7 copy.42
  138.3 3.5 %all-to-all-start.7 = ((bf16[16,32,256]{2,1,0:T(8,128)(2,1)}), bf16[16,32,256]{2,1,0:T(8,128)(2,1)S(1)}, u32[]{:S(2)}, u32[]{:S(2)}) async-start(bf16[16,32,256]{2,1,0:T(8,128)(2,1)} %bitcast.110), calls=%async_computation.7 | async-start | bytes 524288 | tf_op jit(solution)/shard_map/all_to_all | solution.py:28
  142.0 7.1 %all-to-all-done.7 = bf16[16,32,256]{2,1,0:T(8,128)(2,1)S(1)} async-done(((bf16[16,32,256]{2,1,0:T(8,128)(2,1)}), bf16[16,32,256]{2,1,0:T(8,128)(2,1)S(1)}, u32[]{:S(2)}, u32[]{:S(2)}) %all-to-all-start.7) | async-done | bytes 262176 | tf_op jit(solution)/shard_map/all_to_all | solution.py:28
  149.2 14.6 %collective-permute-start.1 = (bf16[32,256]{1,0:T(8,128)(2,1)S(1)}, bf16[32,256]{1,0:T(8,128)(2,1)S(1)}, u32[]{:S(2)}, u32[]{:S(2)}) collective-permute-start(bf16[32,256]{1,0:T(8,128)(2,1)S(1)} %fusion.10), channel_id=1, source_target_pairs={{0,256},{256,0},{1,257},{257,1},{2,258},{258,2},{3,259},{259,3},{4... | collective-permute-start | bytes 49160 | tf_op jit(solution)/shard_map/ppermute | solution.py:24
  163.8 0.6 fusion.19
  164.4 0.6 collective-permute-done.1
  165.1 14.1 %all_to_all.89 = bf16[8,32,256]{2,1,0:T(8,128)(2,1)S(1)} all-to-all(bf16[8,32,256]{2,1,0:T(8,128)(2,1)S(1)} %broadcast_in_dim.141), channel_id=1, replica_groups=mesh['mid'=2,'low'=2,'z'=4,'core'=2,'x'=4,'y'=4] {'z','core'}, dimensions={0} | all-to-all | bytes 262144 | tf_op jit(solution)/shard_map/all_to_all | solution.py:28
  179.1 0.3 convolution_convert_fusion.2
  179.4 10.5 %all_to_all.90 = bf16[16,32,256]{2,1,0:T(8,128)(2,1)S(1)} all-to-all(bf16[16,32,256]{2,1,0:T(8,128)(2,1)S(1)} %bitcast.129), channel_id=1, replica_groups=mesh['mid'=2,'low'=2,'z'=4,'core'=2,'x'=4,'y'=4] {'x','y'}, dimensions={0} | all-to-all | bytes 524288 | tf_op jit(solution)/shard_map/all_to_all | solution.py:28
  190.0 0.7 broadcast_in_dim.142
  190.8 3.8 %all-to-all-start.10 = ((bf16[16,32,256]{2,1,0:T(8,128)(2,1)}), bf16[16,32,256]{2,1,0:T(8,128)(2,1)S(1)}, u32[]{:S(2)}, u32[]{:S(2)}) async-start(bf16[16,32,256]{2,1,0:T(8,128)(2,1)} %broadcast_in_dim.142), calls=%async_computation.10 | async-start | bytes 524288 | tf_op jit(solution)/shard_map/all_to_all | solution.py:28
  194.6 0.7 slice_bitcast_fusion.1.ready_ref
  195.3 6.6 %all-to-all-done.10.recv_ref = bf16[16,32,256]{2,1,0:T(8,128)(2,1)S(1)} async-done(((bf16[16,32,256]{2,1,0:T(8,128)(2,1)}), bf16[16,32,256]{2,1,0:T(8,128)(2,1)S(1)}, u32[]{:S(2)}, u32[]{:S(2)}) %all-to-all-start.10) | async-done | bytes 262176 | tf_op jit(solution)/shard_map/all_to_all | solution.py:28
  201.9 0.9 shard_map.148
  202.8 12.2 %all_to_all.91.recv_ref = bf16[8,40,256]{2,1,0:T(8,128)(2,1)S(1)} all-to-all(bf16[8,40,256]{2,1,0:T(8,128)(2,1)S(1)} %shard_map.148), channel_id=1, replica_groups=mesh['mid'=2,'low'=2,'z'=4,'core'=2,'x'=4,'y'=4] {'z','core'}, dimensions={0} | all-to-all | bytes 327680 | tf_op jit(solution)/shard_map/all_to_all | solution.py:28
  215.0 0.6 shard_map.149
  215.7 10.5 %all_to_all.92.recv_ref = bf16[16,32,256]{2,1,0:T(8,128)(2,1)S(1)} all-to-all(bf16[16,32,256]{2,1,0:T(8,128)(2,1)S(1)} %get-tuple-element.20), channel_id=1, replica_groups=mesh['mid'=2,'low'=2,'z'=4,'core'=2,'x'=4,'y'=4] {'x','y'}, dimensions={0} | all-to-all | bytes 524288 | tf_op jit(solution)/shard_map/all_to_all | solution.py:28
  226.2 1.7 copy-done.3
  227.8 2.1 shard_map.150
  230.0 3.5 %all-to-all-start.13 = ((bf16[16,32,256]{2,1,0:T(8,128)(2,1)}), bf16[16,32,256]{2,1,0:T(8,128)(2,1)S(1)}, u32[]{:S(2)}, u32[]{:S(2)}) async-start(bf16[16,32,256]{2,1,0:T(8,128)(2,1)} %shard_map.150), calls=%async_computation.13 | async-start | bytes 524288 | tf_op jit(solution)/shard_map/all_to_all | solution.py:28
  233.5 0.7 slice_bitcast_fusion.ready_ref
  234.2 19.3 %all-gather.13.cloned.1.call-done = bf16[2048,512]{1,0:T(8,128)(2,1)} async-done(((bf16[256,512]{1,0:T(8,128)(2,1)}), bf16[2048,512]{1,0:T(8,128)(2,1)}) %all-gather.13.cloned.1.call-update) | async-done | bytes 2097168 | tf_op jit(solution)/shard_map/all_gather | solution.py:362
  253.5 1.6 copy-done.4
  255.1 1.4 shard_map.151
  256.5 13.8 %all_to_all.93.recv_ref = bf16[16,32,256]{2,1,0:T(8,128)(2,1)S(1)} all-to-all(bf16[16,32,256]{2,1,0:T(8,128)(2,1)S(1)} %get-tuple-element.23), channel_id=1, replica_groups=mesh['mid'=2,'low'=2,'z'=4,'core'=2,'x'=4,'y'=4] {'x','y'}, dimensions={0} | all-to-all | bytes 524288 | tf_op jit(solution)/shard_map/all_to_all | solution.py:28
  270.3 2.2 copy-done.1
  272.5 1.4 shard_map.152
  273.9 10.7 %all_to_all.94.recv_ref = bf16[16,32,256]{2,1,0:T(8,128)(2,1)S(1)} all-to-all(bf16[16,32,256]{2,1,0:T(8,128)(2,1)S(1)} %shard_map.152), channel_id=1, replica_groups=mesh['mid'=2,'low'=2,'z'=4,'core'=2,'x'=4,'y'=4] {'x','y'}, dimensions={0} | all-to-all | bytes 524288 | tf_op jit(solution)/shard_map/all_to_all | solution.py:28
  284.6 1.5 shard_map.153
  286.1 12.5 %all_to_all.95.recv_ref = bf16[8,8,256]{2,1,0:T(8,128)(2,1)S(1)} all-to-all(bf16[8,8,256]{2,1,0:T(8,128)(2,1)S(1)} %shard_map.153), channel_id=1, replica_groups=mesh['mid'=2,'low'=2,'z'=4,'core'=2,'x'=4,'y'=4] {'z','core'}, dimensions={0} | all-to-all | bytes 65536 | tf_op jit(solution)/shard_map/all_to_all | solution.py:28
  298.6 1.2 shard_map.154
  299.8 1.9 fusion.2
  301.7 1.0 copy.34
  (66 shorter events, 1.6 us)
Async XLA Ops:
  7.2 4.9 %copy-start = (bf16[1024,1024]{1,0:T(8,128)(2,1)S(1)}, bf16[1024,1024]{1,0:T(8,128)(2,1)}, u32[]{:S(2)}) copy-start(bf16[1024,1024]{1,0:T(8,128)(2,1)} %param.13) | copy-start | bytes 6291460
  7.2 84.7 %all-gather.9.cloned.1.call-start = ((), (), s32[]{:S(2)}) async-start(), calls=%async_computation.17 | async-start | bytes 2949120 | tf_op jit(solution)/shard_map/all_gather | solution.py:346
  12.1 1.8 copy-start.9
  12.1 1.8 copy-start.10
  12.1 17.3 %copy-start.5 = (bf16[8,1,32,512]{3,2,1,0:T(8,128)(2,1)S(1)}, bf16[8,1,32,512]{3,2,1,0:T(8,128)(2,1)}, u32[]{:S(2)}) copy-start(bf16[8,1,32,512]{3,2,1,0:T(8,128)(2,1)} %param.20) | copy-start | bytes 786436
  14.0 15.5 %copy-start.6 = (bf16[1024,256]{1,0:T(8,128)(2,1)}, bf16[1024,256]{1,0:T(8,128)(2,1)S(1)}, u32[]{:S(2)}) copy-start(bf16[1024,256]{1,0:T(8,128)(2,1)S(1)} %convolution_convert_fusion.1) | copy-start | bytes 1572868
  14.0 34.2 %copy-start.8 = (bf16[8,1,32,2,256]{4,3,2,1,0:T(2,128)(2,1)S(1)}, bf16[8,1,32,2,256]{4,3,2,1,0:T(2,128)(2,1)}, u32[]{:S(2)}) copy-start(bf16[8,1,32,2,256]{4,3,2,1,0:T(2,128)(2,1)} %param.22) | copy-start | bytes 786436
  29.8 45.9 %copy-start.12 = (bf16[16,256]{1,0:T(8,128)(2,1)S(1)}, bf16[16,256]{1,0:T(8,128)(2,1)}, u32[]{:S(2)}) copy-start(bf16[16,256]{1,0:T(8,128)(2,1)} %param.16) | copy-start | bytes 24580
  29.8 53.2 %copy-start.11 = (bf16[8,256]{1,0:T(8,128)(2,1)S(1)}, bf16[8,256]{1,0:T(8,128)(2,1)}, u32[]{:S(2)}) copy-start(bf16[8,256]{1,0:T(8,128)(2,1)} %param.15) | copy-start | bytes 12292
  42.6 28.1 %all-to-all-start.2 = ((bf16[8,32,256]{2,1,0:T(8,128)(2,1)}), bf16[8,32,256]{2,1,0:T(8,128)(2,1)S(1)}, u32[]{:S(2)}, u32[]{:S(2)}) async-start(bf16[8,32,256]{2,1,0:T(8,128)(2,1)} %broadcast_in_dim.133), calls=%async_computation.2 | async-start | bytes 262144 | tf_op jit(solution)/shard_map/all_to_all | solution.py:28
  71.9 11.0 %all-to-all-start.3 = ((bf16[16,32,256]{2,1,0:T(8,128)(2,1)}), bf16[16,32,256]{2,1,0:T(8,128)(2,1)S(1)}, u32[]{:S(2)}, u32[]{:S(2)}) async-start(bf16[16,32,256]{2,1,0:T(8,128)(2,1)} %bitcast.20), calls=%async_computation.3 | async-start | bytes 524288 | tf_op jit(solution)/shard_map/all_to_all | solution.py:28
  75.5 119.1 %all-gather.11.cloned.1.call-start = ((), (), s32[]{:S(2)}) async-start(), calls=%async_computation.18 | async-start | bytes 2359296 | tf_op jit(solution)/shard_map/all_gather | solution.py:361
  83.1 8.8 %collective-permute-start = (bf16[40,256]{1,0:T(8,128)(2,1)S(1)}, bf16[40,256]{1,0:T(8,128)(2,1)S(1)}, u32[]{:S(2)}, u32[]{:S(2)}) collective-permute-start(bf16[40,256]{1,0:T(8,128)(2,1)S(1)} %pad_maximum_fusion.2), channel_id=1, source_target_pairs={{0,128},{128,0},{1,129},{129,1},{2,130},{130,2},{3,131},{131,3},{4... | collective-permute-start | bytes 61448 | tf_op jit(solution)/shard_map/ppermute | solution.py:24
  91.9 1.7 copy-start.2
  95.3 138.2 %all-gather.15.cloned.1.call-start = ((), (), s32[]{:S(2)}) async-start(), calls=%async_computation.20 | async-start | bytes 4718592 | tf_op jit(solution)/shard_map/all_gather | solution.py:365
  123.2 13.1 %all-to-all-start.6 = ((bf16[8,32,256]{2,1,0:T(8,128)(2,1)}), bf16[8,32,256]{2,1,0:T(8,128)(2,1)S(1)}, u32[]{:S(2)}, u32[]{:S(2)}) async-start(bf16[8,32,256]{2,1,0:T(8,128)(2,1)} %broadcast_in_dim.140), calls=%async_computation.6 | async-start | bytes 262144 | tf_op jit(solution)/shard_map/all_to_all | solution.py:28
  128.8 124.7 %all-gather.13.cloned.1.call-start = ((), (), s32[]{:S(2)}) async-start(), calls=%async_computation.19 | async-start | bytes 2359296 | tf_op jit(solution)/shard_map/all_gather | solution.py:362
  138.3 10.8 %all-to-all-start.7 = ((bf16[16,32,256]{2,1,0:T(8,128)(2,1)}), bf16[16,32,256]{2,1,0:T(8,128)(2,1)S(1)}, u32[]{:S(2)}, u32[]{:S(2)}) async-start(bf16[16,32,256]{2,1,0:T(8,128)(2,1)} %bitcast.110), calls=%async_computation.7 | async-start | bytes 524288 | tf_op jit(solution)/shard_map/all_to_all | solution.py:28
  149.2 15.7 %collective-permute-start.1 = (bf16[32,256]{1,0:T(8,128)(2,1)S(1)}, bf16[32,256]{1,0:T(8,128)(2,1)S(1)}, u32[]{:S(2)}, u32[]{:S(2)}) collective-permute-start(bf16[32,256]{1,0:T(8,128)(2,1)S(1)} %fusion.10), channel_id=1, source_target_pairs={{0,256},{256,0},{1,257},{257,1},{2,258},{258,2},{3,259},{259,3},{4... | collective-permute-start | bytes 49160 | tf_op jit(solution)/shard_map/ppermute | solution.py:24
  190.8 11.1 %all-to-all-start.10 = ((bf16[16,32,256]{2,1,0:T(8,128)(2,1)}), bf16[16,32,256]{2,1,0:T(8,128)(2,1)S(1)}, u32[]{:S(2)}, u32[]{:S(2)}) async-start(bf16[16,32,256]{2,1,0:T(8,128)(2,1)} %broadcast_in_dim.142), calls=%async_computation.10 | async-start | bytes 524288 | tf_op jit(solution)/shard_map/all_to_all | solution.py:28
  226.2 1.7 copy-start.3
  230.0 23.5 %all-to-all-start.13 = ((bf16[16,32,256]{2,1,0:T(8,128)(2,1)}), bf16[16,32,256]{2,1,0:T(8,128)(2,1)S(1)}, u32[]{:S(2)}, u32[]{:S(2)}) async-start(bf16[16,32,256]{2,1,0:T(8,128)(2,1)} %shard_map.150), calls=%async_computation.13 | async-start | bytes 524288 | tf_op jit(solution)/shard_map/all_to_all | solution.py:28
  253.5 1.6 copy-start.4
  270.3 2.2 copy-start.1
  284.6 15.2 %copy-start.7 = (bf16[1024,256]{1,0:T(8,128)(2,1)S(1)}, bf16[1024,256]{1,0:T(8,128)(2,1)}, u32[]{:S(2)}) copy-start(bf16[1024,256]{1,0:T(8,128)(2,1)} %copy-done.6) | copy-start | bytes 1572868
Sparse Core Ops, SparseCore 0:
  10.7 76.3 all-gather.8
  95.4 48.1 all-gather.10
  146.3 62.1 all-gather.14
  210.4 42.9 all-gather.12
